TPU v7x, 32 devices: a whole 2x2x4 slice. The times are simulated.
32 devices in a mesh: group: 2 (over x), tok: 16 (over z, y, core).
Axes of the slice: x: 2, y: 2, z: 4, core: 2. Of those that a mesh axis runs over, the one named last changes fastest.
Arguments:
- initial_guess: float32 [512, 16, 128], P(('group', 'tok')), parts along dimension 0, may hold values from -6 to 6
- noise_draws: float32 [512, 16, 128], P(('group', 'tok')), parts along dimension 0, may hold values from -6 to 6
- drift_state: float32 [16], replicated, may hold values from 0 to 0.15
- drift_denoise: float32 [16], replicated, may hold values from -0.4 to -0.15
- noise_scale: float32 [16], replicated, may hold values from 0.05 to 0.3
- modulation: float32 [16, 8, 1152], replicated, may hold values from -3 to 3
- embed_weight: bfloat16 [16, 1152], replicated, may hold values from -1.5 to 1.5
- space_input: bfloat16 [1152, 1728], replicated, may hold values from -0.1875 to 0.1875
- space_output: bfloat16 [576, 1152], replicated, may hold values from -0.25 to 0.25
- time_input: bfloat16 [1152, 1728], replicated, may hold values from -0.1875 to 0.1875
- time_output: bfloat16 [576, 1152], replicated, may hold values from -0.25 to 0.25
- final_weight: bfloat16 [1152, 16], replicated, may hold values from -0.1875 to 0.1875
Outputs:
- next_states: float32 [512, 16, 128], P(('group', 'tok')), parts along dimension 0
There are 2 independent parts, one for each index of `group`. A program takes and returns all parts, laid end to end along the dimension named above; an argument that names none is the same for every part. Nothing has to cross between parts.
All inputs are finite; a program needn't handle non-finite values.
Results may differ from a plain program's by a relative error of at most 0.006.
Values may be sent and summed in bfloat16 or wider, within the bound.
A program may use at most 128 MiB of HBM per device.

v0:
```python
import functools
import math

import jax
import jax.numpy as jnp
from jax import lax
from jax.experimental import pallas as pl
from jax.experimental.pallas import tpu as pltpu
from jax.sharding import PartitionSpec as P

HEADS = 8
HD = 72
P_SIZE = 16
ITERS = 2
LANES = 128
INNER = HEADS * HD
PADDED = -(-INNER // LANES) * LANES
BLOCK_TOKENS = 256
SIDE = math.isqrt(P_SIZE)


def layer_norm(values):
    center = values - jnp.mean(values, -1, keepdims=True)
    return center * lax.rsqrt(jnp.mean(center * center, -1, keepdims=True) + 1e-06)


def dot_rows(values, weight_rows):
    return lax.dot_general(
        values, weight_rows, (((1,), (1,)), ((), ())), preferred_element_type=jnp.float32
    )


def head_slab(head):
    first = head * HD // LANES
    last = (head * HD + HD - 1) // LANES
    return first, last - first + 1


def part_lanes(part, tile, tiles):
    if part == 1:
        return 1, tile * LANES, (tile + tiles) * LANES
    start = part * INNER
    return 0, start + tile * LANES, start + min((tile + tiles) * LANES, INNER if part else PADDED)


def lined_keys(packed):
    low = INNER // LANES * LANES
    return pltpu.roll(packed[:, low : low + PADDED], PADDED - (INNER - low), 1)


def attend(blocks, rows, keep, lags):
    lane = lax.broadcasted_iota(jnp.int32, (rows, LANES), 1)
    open_tiles = {}
    units = [(head, place) for head in range(HEADS) for place in range(len(blocks))]

    def prepare(unit):
        head, place = unit
        read = blocks[place][0]
        tile, tiles = head_slab(head)
        low = head * HD - tile * LANES
        lanes = lax.broadcasted_iota(jnp.int32, (rows, tiles * LANES), 1)
        inside = (lanes >= low) & (lanes < low + HD)
        queries = jnp.where(inside, read(0, tile, tiles), 0.0)
        keys = jnp.where(inside, read(1, tile, tiles), 0.0)
        query_rate = lax.rsqrt(jnp.sum(queries * queries, -1, keepdims=True) / HD + 1e-06)
        key_rate = lax.rsqrt(jnp.sum(keys * keys, -1, keepdims=True) / HD + 1e-06)
        queries = (queries * (query_rate * (HD**-0.5 * math.log2(math.e)))).astype(jnp.bfloat16)
        return queries, (keys * key_rate).astype(jnp.bfloat16)

    def weigh(unit, prepared):
        weights = jnp.exp2(dot_rows(*prepared))
        if keep is not None:
            weights = jnp.where(keep, weights, 0.0)
        return weights.astype(jnp.bfloat16)

    def mix(unit, weights):
        head, place = unit
        read, write = blocks[place]
        tile, tiles = head_slab(head)
        values = read(2, tile, tiles).astype(jnp.bfloat16)
        ones = jnp.ones((rows, LANES), jnp.bfloat16)
        if tiles == 1:
            values = jnp.concatenate([values, ones], axis=1)
        mixed = jnp.dot(weights, values, preferred_element_type=jnp.float32)
        total = mixed[:, LANES:] if tiles == 1 else jnp.dot(
            weights, ones, preferred_element_type=jnp.float32
        )
        share = 1.0 / total
        for own in range(tile, tile + tiles):
            part = mixed[:, (own - tile) * LANES : min((own - tile + 1) * LANES, values.shape[1])]
            part = part * share[:, : part.shape[1]]
            if (place, own) in open_tiles:
                part = jnp.where(
                    lane >= head * HD - own * LANES, part, open_tiles.pop((place, own))
                )
            if (head + 1) * HD >= min((own + 1) * LANES, INNER):
                write(own, part)
            else:
                open_tiles[place, own] = part

    prepared, weighed = {}, {}
    for at in range(len(units) + lags[1]):
        if at < len(units):
            prepared[at] = prepare(units[at])
        if 0 <= at - lags[0] < len(units):
            weighed[at - lags[0]] = weigh(units[at - lags[0]], prepared.pop(at - lags[0]))
        if 0 <= at - lags[1] < len(units):
            mix(units[at - lags[1]], weighed.pop(at - lags[1]))


def space_kernel(
    step_ref, latent_ref, table_ref, embed_ref, input_ref, output_ref, after_ref,
    embedded_ref, packed_ref, key_ref, mixed_ref,
):
    frames, channels, spatial = latent_ref.shape
    for frame in range(frames):
        embedded_ref[frame * spatial : (frame + 1) * spatial, :] = lax.dot_general(
            latent_ref[frame].astype(jnp.bfloat16),
            embed_ref[...],
            (((0,), (0,)), ((), ())),
            preferred_element_type=jnp.float32,
        )
    normed = (
        layer_norm(embedded_ref[...]) * (1.0 + table_ref[1:2, :]) + table_ref[0:1, :]
    ).astype(jnp.bfloat16)
    packed = dot_rows(normed, input_ref[...])
    packed_ref[...] = packed
    key_ref[...] = lined_keys(packed)

    def one(frame):
        rows = slice(frame * spatial, (frame + 1) * spatial)

        def read(part, tile, tiles):
            source, start, stop = part_lanes(part, tile, tiles)
            return (packed_ref, key_ref)[source][rows, start:stop]

        def write(tile, values):
            mixed_ref[rows, tile * LANES : tile * LANES + values.shape[1]] = values

        return read, write

    attend([one(frame) for frame in range(frames)], spatial, None, (3, 6))
    result = jnp.dot(
        mixed_ref[...].astype(jnp.bfloat16), output_ref[...], preferred_element_type=jnp.float32
    )
    after = (embedded_ref[...] + table_ref[2:3, :] * result).astype(jnp.bfloat16)
    after_ref[...] = after.reshape(after_ref.shape)


def time_kernel(fused, *refs):
    step_ref, after_ref, table_ref, input_ref, output_ref, final_ref, *refs = refs
    if fused:
        latent_ref, noise_ref, *rate_refs, increment_ref, sent_ref = refs[:7]
    else:
        result_ref = refs[0]
    predicted_ref, packed_ref, key_ref, mixed_ref = refs[-4:]
    frames, positions, width = after_ref.shape
    chunk = 8
    tokens = frames * positions
    rows = frames * chunk
    hidden = after_ref[...].reshape(tokens, width).astype(jnp.float32)
    normed = (layer_norm(hidden) * (1.0 + table_ref[4:5, :]) + table_ref[3:4, :]).astype(
        jnp.bfloat16
    )
    packed = dot_rows(normed, input_ref[...])
    packed_ref[...] = packed.reshape(packed_ref.shape)
    key_ref[...] = lined_keys(packed).reshape(key_ref.shape)
    keep = (lax.broadcasted_iota(jnp.int32, (rows, rows), 0) % chunk) == (
        lax.broadcasted_iota(jnp.int32, (rows, rows), 1) % chunk
    )

    def one(index):
        own = slice(index * chunk, (index + 1) * chunk)

        def read(part, tile, tiles):
            source, start, stop = part_lanes(part, tile, tiles)
            return (packed_ref, key_ref)[source][:, own, start:stop].reshape(rows, stop - start)

        def write(tile, values):
            lanes = values.shape[1]
            mixed_ref[:, own, tile * LANES : tile * LANES + lanes] = values.reshape(
                frames, chunk, lanes
            )

        return read, write

    attend([one(index) for index in range(positions // chunk)], rows, keep, (4, 8))
    mixed = mixed_ref[...].reshape(tokens, INNER).astype(jnp.bfloat16)
    result = jnp.dot(mixed, output_ref[...], preferred_element_type=jnp.float32)
    hidden = after_ref[...].reshape(tokens, width).astype(jnp.float32)
    settled = (hidden + table_ref[5:6, :] * result).astype(jnp.bfloat16).astype(jnp.float32)
    normed = (layer_norm(settled) * (1.0 + table_ref[7:8, :]) + table_ref[6:7, :]).astype(
        jnp.bfloat16
    )
    predicted = dot_rows(normed, final_ref[...])
    own = pl.ds(pl.multiple_of(pl.program_id(0) * positions, positions), positions)
    predicted_ref[:, own, :] = predicted.reshape(frames, positions, predicted.shape[1])

    @pl.when(pl.program_id(0) == pl.num_programs(0) - 1)
    def _():
        if fused:
            timestep = step_ref[0]
            rate_state, rate_denoise, rate_noise = (ref[timestep] for ref in rate_refs)
            rate_state = rate_state + jnp.where(timestep == 0, 1.0, 0.0)
        for frame in range(frames):
            turned = predicted_ref[frame].T
            if fused:
                turned = (
                    rate_state * latent_ref[frame]
                    + rate_denoise * turned
                    + rate_noise * noise_ref[frame]
                )
                increment_ref[frame] = turned
                sent_ref[frame] = turned.astype(jnp.bfloat16)
            else:
                result_ref[frame] = turned


def whole(array):
    zeros = (0,) * array.ndim
    return pl.BlockSpec(array.shape, lambda step, *_: zeros, pipeline_mode=pl.Buffered(1))


def own_row(modulation):
    return pl.BlockSpec(
        (None,) + modulation.shape[1:],
        lambda step, own: (own[0], 0, 0),
        pipeline_mode=pl.Buffered(1),
    )


def cost_of(tokens, *weights):
    return pl.CostEstimate(
        flops=2 * tokens * sum(weight.size for weight in weights),
        bytes_accessed=2 * sum(weight.size for weight in weights) + 4 * tokens * weights[0].shape[-1],
        transcendentals=0,
    )


def space_block(own, latent, modulation, embed_weight, input_weight, output_weight):
    frames, channels, spatial = latent.shape
    width = embed_weight.shape[1]
    step_frames = math.gcd(frames, max(1, BLOCK_TOKENS // spatial))
    tokens = step_frames * spatial
    return pl.pallas_call(
        space_kernel,
        out_shape=jax.ShapeDtypeStruct((frames, spatial, width), jnp.bfloat16),
        grid_spec=pltpu.PrefetchScalarGridSpec(
            num_scalar_prefetch=1,
            grid=(frames // step_frames,),
            in_specs=[
                pl.BlockSpec((step_frames, channels, spatial), lambda step, own: (step, 0, 0)),
                own_row(modulation),
                whole(embed_weight),
                whole(input_weight),
                whole(output_weight),
            ],
            out_specs=pl.BlockSpec((step_frames, spatial, width), lambda step, own: (step, 0, 0)),
            scratch_shapes=[
                pltpu.VMEM((tokens, width), jnp.float32),
                pltpu.VMEM((tokens, 3 * INNER), jnp.float32),
                pltpu.VMEM((tokens, PADDED), jnp.float32),
                pltpu.VMEM((tokens, INNER), jnp.float32),
            ],
        ),
        compiler_params=pltpu.CompilerParams(vmem_limit_bytes=60 * 1024 * 1024),
        cost_estimate=cost_of(frames * spatial, input_weight, output_weight, output_weight),
        name="space_block",
    )(own, latent, modulation, embed_weight, input_weight, output_weight)


def time_block(own, after, modulation, input_weight, output_weight, final_weight, fused=()):
    frames, positions, width = after.shape
    channels = final_weight.shape[0]
    step_positions = math.gcd(positions, max(16, BLOCK_TOKENS // frames))
    shape = (frames, channels, positions)
    kinds = [jnp.float32] + [jnp.bfloat16] * bool(fused)
    return pl.pallas_call(
        functools.partial(time_kernel, bool(fused)),
        out_shape=[jax.ShapeDtypeStruct(shape, kind) for kind in kinds],
        grid_spec=pltpu.PrefetchScalarGridSpec(
            num_scalar_prefetch=1,
            grid=(positions // step_positions,),
            in_specs=[
                pl.BlockSpec((frames, step_positions, width), lambda step, own: (0, step, 0)),
                own_row(modulation),
                whole(input_weight),
                whole(output_weight),
                whole(final_weight),
            ]
            + [
                whole(array) if array.ndim > 1 else pl.BlockSpec(memory_space=pltpu.SMEM)
                for array in fused
            ],
            out_specs=[
                pl.BlockSpec(shape, lambda step, own: (0, 0, 0), pipeline_mode=pl.Buffered(1))
                for kind in kinds
            ],
            scratch_shapes=[
                pltpu.VMEM((frames, positions, channels), jnp.float32),
                pltpu.VMEM((frames, step_positions, 3 * INNER), jnp.float32),
                pltpu.VMEM((frames, step_positions, PADDED), jnp.float32),
                pltpu.VMEM((frames, step_positions, INNER), jnp.float32),
            ],
        ),
        compiler_params=pltpu.CompilerParams(vmem_limit_bytes=60 * 1024 * 1024),
        cost_estimate=cost_of(frames * positions, input_weight, output_weight, output_weight),
        name="time_block",
    )(own, after, modulation, input_weight, output_weight, final_weight, *fused)


def carry_kernel(
    last, groups, sent_ref, increment_ref, latent_ref, out_ref,
    part_ref, total_ref, plane_ref, early_ref, stage_ref, before_ref,
    part_send, part_recv, plane_send, plane_recv, stage_send, stage_recv,
):
    quarter = part_ref.shape[1]
    own = lax.axis_index("tok")
    timestep = own // groups
    plane, seat = timestep // SIDE, timestep % SIDE

    def device(plane, seat):
        return {"tok": (plane * SIDE + seat) * groups + own % groups}

    def seat_after(hop):
        return (seat + hop) % SIDE

    barrier = pltpu.get_barrier_semaphore()
    for hop in range(1, SIDE):
        for target in (device(plane, seat_after(hop)), device((plane + hop) % SIDE, seat)):
            pl.semaphore_signal(
                barrier, inc=1, device_id=target, device_id_type=pl.DeviceIdType.MESH
            )
    pl.semaphore_wait(barrier, 2 * (SIDE - 1))

    def copy(source, target, send, receive, to):
        return pltpu.make_async_remote_copy(
            src_ref=source,
            dst_ref=target,
            send_sem=send,
            recv_sem=receive,
            device_id=to,
            device_id_type=pl.DeviceIdType.MESH,
        )

    def rows_of(index):
        return pl.ds(pl.multiple_of(index * quarter, quarter), quarter)

    parts = []
    for hop in range(1, SIDE):
        seat_to = seat_after(hop)
        parts.append(
            copy(
                sent_ref.at[rows_of(seat_to)], part_ref.at[hop - 1],
                part_send.at[hop - 1], part_recv.at[hop - 1], device(plane, seat_to),
            )
        )
        parts[-1].start()
    held = [sent_ref[rows_of(seat)].astype(jnp.float32)]
    for hop in range(1, SIDE):
        parts[hop - 1].wait_recv()
        held.append(part_ref[hop - 1].astype(jnp.float32))
    total_ref[...] = functools.reduce(jnp.add, held).astype(jnp.bfloat16)
    planes = [
        copy(
            total_ref, plane_ref.at[hop - 1], plane_send.at[hop - 1], plane_recv.at[hop - 1],
            device((plane + hop) % SIDE, seat),
        )
        for hop in range(1, SIDE)
    ]
    for hop in range(1, SIDE):
        pl.when(plane + hop < SIDE)(planes[hop - 1].start)

    def earlier_seats(limit):
        total = jnp.zeros_like(held[0])
        for hop in range(SIDE):
            total = total + jnp.where((seat + SIDE - hop) % SIDE < limit, held[hop], 0.0)
        return total

    early_ref[...] = jnp.zeros_like(early_ref)
    for hop in range(1, SIDE):

        @pl.when(plane >= hop)
        def _(hop=hop):
            planes[hop - 1].wait_recv()
            early_ref[...] += plane_ref[hop - 1].astype(jnp.float32)

    early = early_ref[...]
    stages = []
    for hop in range(1, SIDE):
        seat_to = seat_after(hop)
        stage_ref[hop - 1] = early + earlier_seats(seat_to)
        stages.append(
            copy(
                stage_ref.at[hop - 1], before_ref.at[rows_of(seat)],
                stage_send.at[hop - 1], stage_recv.at[hop - 1], device(plane, seat_to),
            )
        )
        stages[-1].start()
    own_rows = rows_of(seat)

    def settle(rows, before):
        if last:
            out_ref[rows] = before + increment_ref[rows]
        else:
            out_ref[rows] = jnp.where(timestep == 0, latent_ref[rows], before)

    settle(own_rows, early + earlier_seats(seat))
    for hop in range(1, SIDE):
        stages[hop - 1].wait_recv()
        rows = rows_of((seat + SIDE - hop) % SIDE)
        settle(rows, before_ref[rows])
    for hop in range(1, SIDE):
        parts[hop - 1].wait_send()
        pl.when(plane + hop < SIDE)(planes[hop - 1].wait_send)
        stages[hop - 1].wait_send()


def carried_kernel(last, groups, sent, increment, latent):
    rows, lanes = sent.shape
    quarter = rows // SIDE
    hops = SIDE - 1
    vmem = pl.BlockSpec(memory_space=pltpu.VMEM)
    return pl.pallas_call(
        functools.partial(carry_kernel, last, groups),
        out_shape=jax.ShapeDtypeStruct((rows, lanes), jnp.float32),
        in_specs=[vmem] * 3,
        out_specs=vmem,
        scratch_shapes=[
            pltpu.VMEM((hops, quarter, lanes), jnp.bfloat16),
            pltpu.VMEM((quarter, lanes), jnp.bfloat16),
            pltpu.VMEM((hops, quarter, lanes), jnp.bfloat16),
            pltpu.VMEM((quarter, lanes), jnp.float32),
            pltpu.VMEM((hops, quarter, lanes), jnp.float32),
            pltpu.VMEM((rows, lanes), jnp.float32),
        ]
        + [pltpu.SemaphoreType.DMA((hops,))] * 6,
        compiler_params=pltpu.CompilerParams(collective_id=int(last), has_side_effects=True),
        name="carry_last" if last else "carry",
    )(sent, increment, latent)


def carried_in(last, groups, same_block, timestep, sent, increment, latent):
    rows = sent.size // LANES
    if sent.shape[-1] == LANES and rows % (SIDE * 16) == 0:
        flat = [array.reshape(rows, LANES) for array in (sent, increment, latent)]
        return carried_kernel(last, groups, *flat).reshape(latent.shape)
    gathered = lax.all_gather(
        sent, "tok", axis_index_groups=same_block if groups > 1 else None
    )
    earlier = (jnp.arange(P_SIZE) < timestep)[:, None, None, None]
    before = jnp.sum(jnp.where(earlier, gathered.astype(jnp.float32), 0.0), axis=0)
    return before + increment if last else jnp.where(timestep == 0, latent, before)


def body(
    initial_guess,
    noise_draws,
    drift_state,
    drift_denoise,
    noise_scale,
    modulation,
    embed_weight,
    space_input,
    space_output,
    time_input,
    time_output,
    final_weight,
):
    devices = lax.axis_size("tok")
    own_index = lax.axis_index("tok")
    groups = devices // P_SIZE
    timestep = own_index // groups
    own = jnp.reshape(timestep, (1,)).astype(jnp.int32)
    rates = (drift_state, drift_denoise, noise_scale)
    same_step = [[step * groups + block for block in range(groups)] for step in range(P_SIZE)]
    same_block = [[step * groups + block for step in range(P_SIZE)] for block in range(groups)]
    space_input, time_input, final_weight = space_input.T, time_input.T, final_weight.T
    latent = initial_guess
    for iteration in range(ITERS):
        after = space_block(own, latent, modulation, embed_weight, space_input, space_output)
        if groups == 1:
            increment, sent = time_block(
                own, after, modulation, time_input, time_output, final_weight,
                (latent, noise_draws) + rates,
            )
        else:
            after = lax.all_to_all(
                after, "tok", split_axis=1, concat_axis=0, axis_index_groups=same_step, tiled=True
            )
            (predicted,) = time_block(own, after, modulation, time_input, time_output, final_weight)
            predicted = lax.all_to_all(
                predicted, "tok", split_axis=0, concat_axis=2, axis_index_groups=same_step, tiled=True
            )
            rate_state, rate_denoise, rate_noise = (
                lax.dynamic_index_in_dim(rate, timestep, 0, keepdims=False) for rate in rates
            )
            rate_state = rate_state + jnp.where(timestep == 0, 1.0, 0.0)
            increment = rate_state * latent + rate_denoise * predicted + rate_noise * noise_draws
            sent = increment.astype(jnp.bfloat16)
        latent = carried_in(
            iteration == ITERS - 1, groups, same_block, timestep, sent, increment, latent
        )
    return latent


def solution(mesh):
    placed = (
        P(("group", "tok"), None, None),
        P(("group", "tok"), None, None),
        P(),
        P(),
        P(),
        P(),
        P(),
        P(),
        P(),
        P(),
        P(),
        P(),
    )
    return jax.shard_map(
        body, mesh=mesh, in_specs=placed, out_specs=P(("group", "tok"), None, None), check_vma=False
    )
```

profile of v0, /device:TPU:0, one launch (start us, length us, event | category | flops | bytes accessed | tf_op | source)
XLA Modules:
  0.0 155.8 jit_solution(6933351060187633769)
XLA Ops:
  0.0 29.0 %space_block.2.refs_1_ = bf16[16,128,1152]{2,1,0:T(8,128)(2,1)} custom-call(s32[1]{0:T(128)} %bitcast.step_ref.refs_0_, f32[16,16,128]{2,1,0:T(8,128)} %refs_6_.1, f32[16,8,1152]{2,1,0:T(8,128)} %refs_2_.3, bf16[16,1152]{1,0:T(8,128)(2,1)} %embed_ref.3, bf16[1728,1152]{1,0:T(8,128)(2,1)} %bitcast.19, bf16[576,1152]{1,0:T(8,128)(2,1)} %output_ref.3), custom_call_target="tpu_custom_call" | custom-call | flops 13589544960 | bytes 16072704 | tf_op jit(solution)/shard_map/space_block/pallas_call | solution.py:245
  29.0 35.0 %time_block.2 = (f32[16,16,128]{2,1,0:T(8,128)}, bf16[16,16,128]{2,1,0:T(8,128)(2,1)}) custom-call(s32[1]{0:T(128)} %bitcast.step_ref.refs_0_, bf16[16,128,1152]{2,1,0:T(8,128)(2,1)} %space_block.2.refs_1_, f32[16,8,1152]{2,1,0:T(8,128)} %refs_2_.3, bf16[1728,1152]{1,0:T(8,128)(2,1)} %bitcast.21, bf16[576,1152]{1,0:T(8,128)(2,1)} %refs_4_.3, ...), custom_call_target="tpu_custom_call" | custom-call | flops 13589544960 | bytes 16072704 | tf_op jit(solution)/shard_map/time_block/pallas_call | solution.py:278
  64.0 12.9 %carry.1.latent_ref = f32[256,128]{1,0:T(8,128)} custom-call(bf16[256,128]{1,0:T(8,128)(2,1)} %bitcast.18, f32[256,128]{1,0:T(8,128)} %bitcast.16, f32[256,128]{1,0:T(8,128)} %bitcast.14), custom_call_target="tpu_custom_call" | custom-call | tf_op jit(solution)/shard_map/carry/pallas_call | solution.py:424
  76.9 29.1 %space_block.3.refs_1_ = bf16[16,128,1152]{2,1,0:T(8,128)(2,1)} custom-call(s32[1]{0:T(128)} %bitcast.step_ref.refs_0_, f32[16,16,128]{2,1,0:T(8,128)} %bitcast.11, f32[16,8,1152]{2,1,0:T(8,128)} %refs_2_.3, bf16[16,1152]{1,0:T(8,128)(2,1)} %embed_ref.3, bf16[1728,1152]{1,0:T(8,128)(2,1)} %bitcast.20, bf16[576,1152]{1,0:T(8,128)(2,1)} %output_ref.3), custom_call_target="tpu_custom_call" | custom-call | flops 13589544960 | bytes 16072704 | tf_op jit(solution)/shard_map/space_block/pallas_call | solution.py:245
  106.0 35.0 %time_block.3 = (f32[16,16,128]{2,1,0:T(8,128)}, bf16[16,16,128]{2,1,0:T(8,128)(2,1)}) custom-call(s32[1]{0:T(128)} %bitcast.step_ref.refs_0_, bf16[16,128,1152]{2,1,0:T(8,128)(2,1)} %space_block.3.refs_1_, f32[16,8,1152]{2,1,0:T(8,128)} %refs_2_.3, bf16[1728,1152]{1,0:T(8,128)(2,1)} %bitcast.22, bf16[576,1152]{1,0:T(8,128)(2,1)} %refs_4_.3, ...), custom_call_target="tpu_custom_call" | custom-call | flops 13589544960 | bytes 16072704 | tf_op jit(solution)/shard_map/time_block/pallas_call | solution.py:278
  141.0 13.2 %carry_last.1 = f32[256,128]{1,0:T(8,128)} custom-call(bf16[256,128]{1,0:T(8,128)(2,1)} %bitcast.17, f32[256,128]{1,0:T(8,128)} %bitcast.15, f32[256,128]{1,0:T(8,128)} %carry.1.latent_ref), custom_call_target="tpu_custom_call" | custom-call | tf_op jit(solution)/shard_map/carry_last/pallas_call | solution.py:424
  154.2 1.6 %copy.14 = f32[16,16,128]{2,1,0:T(8,128)} copy(f32[16,16,128]{2,1,0:T(8,128)} %bitcast.13) | data formatting | bytes 262144
where the time goes:
time: 157 us; the launch traced here: 156 us
  Pallas kernels  154 us (98%)
  local copies, waits for them, and re-layouts  1.57 us (1%)
    pallas_call x2, Pallas kernels, time_block(): pl.pallas_call(functools.partial(time_kernel, bool(fused)), out_shape=[ja...  70 us
    pallas_call x2, Pallas kernels, space_block(): pl.pallas_call(space_kernel, out_shape=jax.ShapeDtypeStruct((frames, spat...  58.1 us
    pallas_call x2, Pallas kernels, carried_kernel(): pl.pallas_call(functools.partial(carry_kernel, last, groups), out_shape=j...  26.1 us

commit v1 on v0

v1 whole, which is shorter than its diff:
```python
import functools
import math

import jax
import jax.numpy as jnp
from jax import lax
from jax.experimental import pallas as pl
from jax.experimental.pallas import tpu as pltpu
from jax.sharding import PartitionSpec as P

HEADS = 8
HD = 72
P_SIZE = 16
ITERS = 2
LANES = 128
INNER = HEADS * HD
SIDE = math.isqrt(P_SIZE)
EPS = 1e-06
CHANNELS = 16
WIDE = 2 * LANES
ROWS_T = HEADS * CHANNELS
ROWS_AA = 3 * ROWS_T + 32
BASE = 512
TAIL = INNER - BASE
V_COLS = BASE + LANES
PACKED = 2 * HEADS * LANES + V_COLS
LAT, DUP, ZERO, ONE, ATT = 128, 144, 160, 184, 192
SCALE = HD**-0.5 * math.log2(math.e)
UNIT = HD**0.5 * math.log2(math.e)


def dot_rows(values, weight_rows, precision=None):
    return lax.dot_general(
        values,
        weight_rows,
        (((1,), (1,)), ((), ())),
        preferred_element_type=jnp.float32,
        precision=precision,
    )


def dot(values, weights):
    return jnp.dot(values, weights, preferred_element_type=jnp.float32)


def halves(values):
    high = values.astype(jnp.bfloat16)
    return high, (values - high.astype(jnp.float32)).astype(jnp.bfloat16)


def lane_of(shape):
    return lax.broadcasted_iota(jnp.int32, shape, len(shape) - 1)


def row_of(shape):
    return lax.broadcasted_iota(jnp.int32, shape, 0)


def centred(rows):
    return rows - jnp.mean(rows, -1, keepdims=True)


def by_head(rows, order):
    count, width = rows.shape
    if order == "hc":
        spread = jnp.concatenate([rows] * HEADS, axis=0)
        head = row_of(spread.shape) // count
    else:
        spread = jnp.broadcast_to(rows[:, None, :], (count, HEADS, width)).reshape(-1, width)
        head = row_of(spread.shape) % HEADS
    return jnp.where(lane_of(spread.shape) // HD == head, spread, 0.0)


def fold_kernel(
    step_ref, table_ref, embed_ref, space_in_ref, space_out_ref, time_in_ref, time_out_ref, final_ref,
    first_ref, offset_ref, packed_ref, square_ref, shift_ref, lines_ref,
):
    def table(row):
        return table_ref[row : row + 1, :]

    def zeros(rows, width=None):
        return jnp.zeros((rows, width or table_ref.shape[1]), jnp.float32)

    highest = lax.Precision.HIGHEST
    features = table_ref.shape[1]
    embed = centred(embed_ref[...].astype(jnp.float32))
    lines = embed * (1.0 + table(1))
    shift = jnp.concatenate([table(0), zeros(7)], axis=0)
    high, low = halves(lines)
    shift_high, shift_low = halves(shift)
    tail = jnp.concatenate([shift_high.astype(jnp.float32), shift_low.astype(jnp.float32)], axis=0)
    folded = dot_rows(
        jnp.concatenate([high, low, tail.astype(jnp.bfloat16)], axis=0), space_in_ref[...]
    )
    lat = folded[:CHANNELS] + folded[CHANNELS : 2 * CHANNELS]
    const = folded[2 * CHANNELS : 2 * CHANNELS + 8] + folded[2 * CHANNELS + 8 :]

    def part(values, which):
        return values[:, which * INNER : (which + 1) * INNER]

    query, key, value = (part(lat, which) for which in range(3))
    query_c, key_c, value_c = (part(const, which)[:1] for which in range(3))
    key_side = jnp.concatenate([key, key, key_c, zeros(7, INNER)], axis=0)
    query_side = jnp.concatenate([query, query, query_c, zeros(7, INNER)], axis=0)
    scores = dot_rows(
        jnp.concatenate([by_head(query, "hc"), by_head(query_c, "ch")], axis=0) * SCALE,
        key_side, highest,
    )
    key_square = dot_rows(
        jnp.concatenate([by_head(key, "ch"), by_head(key_c, "ch")], axis=0) * (1.0 / HD),
        key_side, highest,
    )
    query_square = dot_rows(
        jnp.concatenate([by_head(query, "ch"), by_head(query_c, "ch")], axis=0) * (1.0 / HD),
        query_side, highest,
    )
    gram = dot_rows(embed, jnp.concatenate([embed, embed, zeros(8)], axis=0), highest) * (
        1.0 / features
    )
    first = jnp.concatenate(
        [scores, key_square[:ROWS_T], query_square[:ROWS_T], gram, zeros(8, 2 * CHANNELS + 8)],
        axis=0,
    )
    high, low = halves(first)
    upper = lane_of(first.shape) < CHANNELS
    chosen = jnp.where(upper, high.astype(jnp.float32), low.astype(jnp.float32))
    first_ref[...] = chosen[:, : 2 * CHANNELS].astype(jnp.bfloat16)
    point = 2 * CHANNELS
    offset_ref[: ROWS_T + 8] = jnp.broadcast_to(scores[:, point : point + 1], (ROWS_T + 8, LANES))
    for index, square in enumerate((key_square, query_square)):
        start = ROWS_T + 8 + index * (ROWS_T + 8)
        offset_ref[start : start + ROWS_T] = jnp.broadcast_to(
            2.0 * square[:ROWS_T, point : point + 1], (ROWS_T, LANES)
        )
        offset_ref[start + ROWS_T : start + ROWS_T + 8] = jnp.broadcast_to(
            square[ROWS_T:, point : point + 1], (8, LANES)
        )

    value_high, value_low = halves(by_head(value, "hc"))
    const_high, const_low = halves(jnp.concatenate([value_c, zeros(7, INNER)], axis=0))
    tail = jnp.concatenate([const_high.astype(jnp.float32), const_low.astype(jnp.float32)], axis=0)
    mixed = dot(
        jnp.concatenate([value_high, value_low, tail.astype(jnp.bfloat16)], axis=0),
        space_out_ref[...],
    )
    gate = table(2)
    attended = centred(gate * (mixed[:ROWS_T] + mixed[ROWS_T : 2 * ROWS_T]))
    point = centred(gate * (mixed[2 * ROWS_T : 2 * ROWS_T + 8] + mixed[2 * ROWS_T + 8 :]))

    scaled = 1.0 + table(4)
    lat_high, lat_low = halves(embed * scaled)
    ends = jnp.concatenate([table(3), point[:1] * scaled, zeros(6)], axis=0)
    ends_high, ends_low = halves(ends)
    tail = jnp.concatenate([ends_high.astype(jnp.float32), ends_low.astype(jnp.float32)], axis=0)
    rows = jnp.concatenate(
        [(attended * scaled).astype(jnp.bfloat16), lat_high, lat_low, tail.astype(jnp.bfloat16)],
        axis=0,
    )

    def settle(columns):
        lat = columns[LAT:DUP] + columns[DUP : DUP + CHANNELS]
        lat_high = lat.astype(jnp.bfloat16).astype(jnp.float32)
        ends = columns[DUP + CHANNELS : DUP + CHANNELS + 8] + columns[DUP + CHANNELS + 8 :]
        ends_high = ends.astype(jnp.bfloat16).astype(jnp.float32)
        ends_low = ends - ends_high
        width = columns.shape[1]
        return jnp.concatenate(
            [
                columns[:LAT], lat_high, lat - lat_high,
                ends_high[:1], ends_high[:1], ends_low[:1], zeros(ONE - ZERO - 3, width),
                ends_high[1:2], ends_low[1:2], zeros(WIDE - ONE - 2, width),
            ],
            axis=0,
        ).astype(jnp.bfloat16)

    packed_ref[...] = jnp.zeros_like(packed_ref)
    for which in range(3):
        columns = settle(dot_rows(rows, time_in_ref[which * INNER : (which + 1) * INNER, :]))
        if which == 2:
            start = 2 * HEADS * LANES
            packed_ref[:, start : start + BASE] = columns[:, :BASE]
            packed_ref[:, start + BASE + LANES - TAIL : start + V_COLS] = columns[:, BASE:]
        else:
            for head in range(HEADS):
                start = (which * HEADS + head) * LANES
                packed_ref[:, start : start + HD] = columns[:, head * HD : (head + 1) * HD]

    gate = table(5)
    lat_high, lat_low = halves(embed)
    point_high, point_low = halves(point[:1])
    lines_ref[:LAT] = attended.astype(jnp.bfloat16)
    lines_ref[LAT:DUP] = lat_high
    lines_ref[DUP:ZERO] = lat_low
    lines_ref[ZERO:ATT] = jnp.concatenate(
        [
            zeros(ONE - ZERO), point_high.astype(jnp.float32), point_low.astype(jnp.float32),
            zeros(ATT - ONE - 2),
        ],
        axis=0,
    ).astype(jnp.bfloat16)
    lines_ref[ATT:WIDE] = centred(gate * time_out_ref[BASE:].astype(jnp.float32)).astype(jnp.bfloat16)
    for start in range(0, BASE, LANES):
        lines_ref[WIDE + start : WIDE + start + LANES] = centred(
            gate * time_out_ref[start : start + LANES].astype(jnp.float32)
        ).astype(jnp.bfloat16)
    final = final_ref[...].astype(jnp.float32)
    shift_ref[...] = jnp.broadcast_to(
        jnp.sum(final * table(6), -1, keepdims=True), (CHANNELS, LANES)
    )
    base = jnp.concatenate(
        [
            lines_ref[:ZERO],
            (final * (1.0 + table(7))).astype(jnp.bfloat16),
            lines_ref[ZERO + CHANNELS : WIDE],
        ],
        axis=0,
    )
    lane = lane_of((1, WIDE))
    plain = (lane >= ZERO) & (lane < ZERO + CHANNELS)
    tiles = lines_ref.shape[0] // WIDE
    for column in range(tiles):
        other = lines_ref[column * WIDE : (column + 1) * WIDE] if column else base
        for row in range(column, tiles):
            block = dot_rows(lines_ref[row * WIDE : (row + 1) * WIDE], other)
            block = block * ((1.0 if row == column else 2.0) / features) if column else (
                block * jnp.where(plain, 1.0, (1.0 if row == column else 2.0) / features)
            )
            square_ref[row * WIDE : (row + 1) * WIDE, column * WIDE : (column + 1) * WIDE] = (
                block.astype(jnp.bfloat16)
            )


def space_kernel(latent_ref, first_ref, offset_ref, token_ref):
    frames, channels, spatial = latent_ref.shape
    bf16 = jnp.bfloat16
    f32 = jnp.float32
    head_lane = lane_of((spatial, LANES)) // CHANNELS
    head_row = row_of((HEADS, spatial))
    kept = lane_of((spatial, 64))
    kept = (kept < 32) | (kept >= 56)

    def offset(start, rows):
        return offset_ref[start : start + rows]

    stacked = []
    for frame in range(frames):
        latent = latent_ref[frame].astype(bf16)
        stacked.append(jnp.concatenate([latent, latent], axis=0))
    product = dot(first_ref[...], jnp.concatenate(stacked, axis=1))
    for frame in range(frames):
        result = product[:, frame * spatial : (frame + 1) * spatial]
        latent = stacked[frame][:channels].astype(f32)
        gram = result[3 * ROWS_T + 8 : 3 * ROWS_T + 8 + channels]
        variance = jnp.maximum(jnp.sum(latent * gram, 0, keepdims=True), 0.0) + EPS
        rate = lax.rsqrt(variance)
        spread = variance * rate
        scaled = latent * rate

        def norm(index):
            start = ROWS_T + 8 + index * ROWS_T
            place = ROWS_T + 8 + index * (ROWS_T + 8)
            terms = rate * result[start : start + ROWS_T] + offset(place, ROWS_T)
            terms = terms.reshape(channels, HEADS, spatial) * scaled[:, None, :]
            total = jnp.sum(terms, 0) + offset(place + ROWS_T, 8)
            return lax.rsqrt(jnp.maximum(total, 0.0) + EPS)

        key_rate, query_rate = norm(0), norm(1)
        query_rate = (query_rate * rate).T
        terms = rate * result[:ROWS_T] + offset(0, ROWS_T)
        point = (rate * result[ROWS_T : ROWS_T + 8] + offset(ROWS_T, 8)) * key_rate
        point_high = point.astype(bf16).astype(f32)
        point_low = point - point_high
        spread = jnp.broadcast_to(spread, (8, spatial))
        spread_high = spread.astype(bf16).astype(f32)
        ends = jnp.concatenate(
            [spread_high, spread - spread_high, spread_high, jnp.ones_like(spread)], axis=0
        ).astype(bf16)
        tokens = jnp.concatenate([stacked[frame], ends], axis=0).T

        def columns(head):
            own = terms[head * channels : (head + 1) * channels] * key_rate[head : head + 1]
            high, low = halves(own)
            mine = head_row == head
            point_mine = jnp.where(mine, point_high, 0.0)
            ends = jnp.concatenate(
                [point_mine, point_mine, jnp.where(mine, point_low, 0.0), jnp.zeros_like(point_mine)],
                axis=0,
            ).astype(bf16)
            return jnp.concatenate([high, low, ends], axis=0)

        spot = jnp.concatenate([scaled] * HEADS, axis=0).astype(bf16).T
        mixed = None
        weights, sources = [], []
        for pair in range(HEADS // 2):
            heads = (2 * pair, 2 * pair + 1)
            score = dot(tokens, jnp.concatenate([columns(head) for head in heads], axis=1))
            for place, head in enumerate(heads):
                own = score[:, place * spatial : (place + 1) * spatial]
                weights.append(jnp.exp2(own * query_rate[:, head : head + 1]).astype(bf16))
                mine = head_lane == head
                sources.append(
                    jnp.concatenate(
                        [
                            jnp.where(mine, spot, jnp.zeros_like(spot)),
                            jnp.where(mine, 1.0, 0.0).astype(bf16),
                        ],
                        axis=1,
                    )
                )
        mixed = dot(jnp.concatenate(weights, axis=1), jnp.concatenate(sources, axis=0))
        average = mixed[:, :LANES] / mixed[:, LANES:]
        token_ref[frame, :, :LANES] = average.astype(bf16)
        token_ref[frame, :, LANES:] = jnp.concatenate(
            [jnp.where(kept, tokens, jnp.zeros_like(tokens)), jnp.zeros_like(tokens)], axis=1
        )


def time_kernel(fused, *refs):
    step_ref, token_ref, packed_ref, square_ref, shift_ref, *refs = refs
    if fused:
        latent_ref, noise_ref, *rate_refs, increment_ref, sent_ref = refs[:7]
    else:
        result_ref = refs[0]
    predicted_ref = refs[-1]
    bf16 = jnp.bfloat16
    f32 = jnp.float32
    frames, positions, width = token_ref.shape
    count = frames * positions
    chunk = 8
    rows = frames * chunk
    tokens = token_ref[...].reshape(count, width)
    variance = jnp.sum(tokens.astype(f32) * dot(tokens, square_ref[:WIDE, :WIDE]), -1, keepdims=True)
    variance = jnp.maximum(variance, 0.0) + EPS
    pace = lax.rsqrt(variance)
    spread = variance * pace
    spread_high = spread.astype(bf16).astype(f32)
    lane = lane_of((count, LANES))
    upper = tokens[:, LANES:].astype(f32)
    upper = jnp.where((lane == ZERO - LANES) | (lane == ZERO - LANES + 2), spread_high, upper)
    upper = jnp.where(lane == ZERO - LANES + 1, spread - spread_high, upper)
    entry = jnp.concatenate([tokens[:, :LANES], upper.astype(bf16)], axis=1)
    packed = dot(entry, packed_ref[...])
    floor = (HD * EPS) * variance
    keep = (row_of((rows, rows)) % chunk) == (lane_of((rows, rows)) % chunk)
    value_lane = lane_of((rows, V_COLS))
    value_lane = jnp.where(value_lane < BASE, value_lane, jnp.where(value_lane < BASE + LANES - TAIL, -1, value_lane - (LANES - TAIL)))
    value_head = jnp.where(value_lane < 0, -1, value_lane // HD)
    parts = positions // chunk

    def of_part(values, part):
        lanes = values.shape[1]
        return values.reshape(frames, parts, chunk, lanes)[:, part].reshape(rows, lanes)

    for part in range(parts):
        own_floor = of_part(floor, part)
        own_tokens = of_part(tokens.astype(f32), part)
        values = of_part(packed[:, 2 * HEADS * LANES :], part) * of_part(pace, part)
        values = values.astype(bf16)

        def slab(which, head, gain):
            start = (which * HEADS + head) * LANES
            own = of_part(packed[:, start : start + LANES], part)
            size = lax.rsqrt(jnp.sum(own * own, -1, keepdims=True) + own_floor)
            return (own * (size * gain if gain else size)).astype(bf16)

        weights = []
        for pair in range(HEADS // 2):
            heads = (2 * pair, 2 * pair + 1)
            query = jnp.concatenate([slab(0, head, UNIT) for head in heads], axis=1)
            key = [slab(1, head, None) for head in heads]
            blank = jnp.zeros_like(key[0])
            keys = jnp.concatenate(
                [jnp.concatenate([key[0], blank], axis=1), jnp.concatenate([blank, key[1]], axis=1)],
                axis=0,
            )
            score = dot_rows(query, keys)
            for place in range(2):
                weight = jnp.where(keep, jnp.exp2(score[:, place * rows : (place + 1) * rows]), 0.0)
                total = jnp.sum(weight, -1, keepdims=True)
                weights.append((weight * (1.0 / total)).astype(bf16))

        def mixed(heads, start, stop):
            source = [
                jnp.where(value_head[:, start:stop] == head, values[:, start:stop], jnp.zeros((), bf16))
                for head in heads
            ]
            return dot(
                jnp.concatenate([weights[head] for head in heads], axis=1),
                jnp.concatenate(source, axis=0),
            )

        def heads_in(start, stop):
            return range(start // HD, (stop - 1) // HD + 1)

        low = mixed(heads_in(0, WIDE), 0, WIDE)
        high = mixed(heads_in(WIDE, BASE), WIDE, BASE)
        tail = mixed(heads_in(BASE, INNER), BASE, V_COLS)
        state = jnp.concatenate(
            [own_tokens[:, :LANES], own_tokens[:, LANES:] + tail, low, high], axis=1
        ).astype(bf16)
        total = jnp.zeros((rows, LANES), f32)
        for column in range(state.shape[1] // WIDE):
            own = slice(column * WIDE, (column + 1) * WIDE)
            block = dot(state[:, column * WIDE :], square_ref[column * WIDE :, own])
            if column == 0:
                predicted = block[:, LANES:]
            for half in range(2):
                lanes = slice(half * LANES, (half + 1) * LANES)
                total = total + block[:, lanes] * state[:, own][:, lanes].astype(f32)
        rate = lax.rsqrt(jnp.maximum(jnp.sum(total, -1, keepdims=True), 0.0) + EPS)
        start = pl.multiple_of(pl.program_id(0) * positions + part * chunk, chunk)
        predicted_ref[:, pl.ds(start, chunk), :] = (predicted * rate).reshape(frames, chunk, LANES)

    @pl.when(pl.program_id(0) == pl.num_programs(0) - 1)
    def _():
        if fused:
            timestep = step_ref[0]
            rate_state, rate_denoise, rate_noise = (ref[timestep] for ref in rate_refs)
            rate_state = rate_state + jnp.where(timestep == 0, 1.0, 0.0)
        for frame in range(frames):
            turned = predicted_ref[frame].T[ZERO - LANES : ZERO - LANES + CHANNELS]
            turned = turned + shift_ref[:, : turned.shape[1]]
            if fused:
                turned = (
                    rate_state * latent_ref[frame]
                    + rate_denoise * turned
                    + rate_noise * noise_ref[frame]
                )
                increment_ref[frame] = turned
                sent_ref[frame] = turned.astype(jnp.bfloat16)
            else:
                result_ref[frame] = turned


def whole(array):
    zeros = (0,) * array.ndim
    return pl.BlockSpec(array.shape, lambda *_: zeros, pipeline_mode=pl.Buffered(1))


def fold(own, modulation, embed_weight, space_input, space_output, time_input, time_output, final_weight):
    features = modulation.shape[2]
    shapes = [
        ((ROWS_AA, 2 * CHANNELS), jnp.bfloat16),
        ((3 * (ROWS_T + 8), LANES), jnp.float32),
        ((WIDE, PACKED), jnp.bfloat16),
        ((BASE + WIDE, BASE + WIDE), jnp.bfloat16),
        ((CHANNELS, LANES), jnp.float32),
    ]
    weights = (embed_weight, space_input, space_output, time_input, time_output, final_weight)
    return pl.pallas_call(
        fold_kernel,
        out_shape=[jax.ShapeDtypeStruct(*shape) for shape in shapes],
        grid_spec=pltpu.PrefetchScalarGridSpec(
            num_scalar_prefetch=1,
            grid=(1,),
            in_specs=[
                pl.BlockSpec(
                    (None,) + modulation.shape[1:],
                    lambda step, own: (own[0], 0, 0),
                    pipeline_mode=pl.Buffered(1),
                )
            ]
            + [whole(weight) for weight in weights],
            out_specs=[
                pl.BlockSpec(shape, lambda *_: (0, 0), pipeline_mode=pl.Buffered(1))
                for shape, kind in shapes
            ],
            scratch_shapes=[pltpu.VMEM((BASE + WIDE, features), jnp.bfloat16)],
        ),
        compiler_params=pltpu.CompilerParams(vmem_limit_bytes=60 * 1024 * 1024),
        name="fold",
    )(own, modulation, *weights)


def space_block(latent, first, offset):
    frames, channels, spatial = latent.shape
    step_frames = math.gcd(frames, 2)
    return pl.pallas_call(
        space_kernel,
        out_shape=jax.ShapeDtypeStruct((frames, spatial, WIDE), jnp.bfloat16),
        grid=(frames // step_frames,),
        in_specs=[
            pl.BlockSpec((step_frames, channels, spatial), lambda step: (step, 0, 0)),
            whole(first),
            whole(offset),
        ],
        out_specs=pl.BlockSpec((step_frames, spatial, WIDE), lambda step: (step, 0, 0)),
        compiler_params=pltpu.CompilerParams(vmem_limit_bytes=60 * 1024 * 1024),
        name="space_block",
    )(latent, first, offset)


def time_block(own, tokens, packed, square, shift, fused=()):
    frames, positions, width = tokens.shape
    step_positions = math.gcd(positions, 16)
    shape = (frames, CHANNELS, positions)
    kinds = [jnp.float32] + [jnp.bfloat16] * bool(fused)
    return pl.pallas_call(
        functools.partial(time_kernel, bool(fused)),
        out_shape=[jax.ShapeDtypeStruct(shape, kind) for kind in kinds],
        grid_spec=pltpu.PrefetchScalarGridSpec(
            num_scalar_prefetch=1,
            grid=(positions // step_positions,),
            in_specs=[
                pl.BlockSpec((frames, step_positions, width), lambda step, own: (0, step, 0)),
                whole(packed),
                whole(square),
                whole(shift),
            ]
            + [
                whole(array) if array.ndim > 1 else pl.BlockSpec(memory_space=pltpu.SMEM)
                for array in fused
            ],
            out_specs=[
                pl.BlockSpec(shape, lambda step, own: (0, 0, 0), pipeline_mode=pl.Buffered(1))
                for kind in kinds
            ],
            scratch_shapes=[pltpu.VMEM((frames, positions, LANES), jnp.float32)],
        ),
        compiler_params=pltpu.CompilerParams(vmem_limit_bytes=60 * 1024 * 1024),
        name="time_block",
    )(own, tokens, packed, square, shift, *fused)


def carry_kernel(
    last, groups, sent_ref, increment_ref, latent_ref, out_ref,
    part_ref, total_ref, plane_ref, early_ref, stage_ref, before_ref,
    part_send, part_recv, plane_send, plane_recv, stage_send, stage_recv,
):
    quarter = part_ref.shape[1]
    own = lax.axis_index("tok")
    timestep = own // groups
    plane, seat = timestep // SIDE, timestep % SIDE

    def device(plane, seat):
        return {"tok": (plane * SIDE + seat) * groups + own % groups}

    def seat_after(hop):
        return (seat + hop) % SIDE

    barrier = pltpu.get_barrier_semaphore()
    for hop in range(1, SIDE):
        for target in (device(plane, seat_after(hop)), device((plane + hop) % SIDE, seat)):
            pl.semaphore_signal(
                barrier, inc=1, device_id=target, device_id_type=pl.DeviceIdType.MESH
            )
    pl.semaphore_wait(barrier, 2 * (SIDE - 1))

    def copy(source, target, send, receive, to):
        return pltpu.make_async_remote_copy(
            src_ref=source,
            dst_ref=target,
            send_sem=send,
            recv_sem=receive,
            device_id=to,
            device_id_type=pl.DeviceIdType.MESH,
        )

    def rows_of(index):
        return pl.ds(pl.multiple_of(index * quarter, quarter), quarter)

    parts = []
    for hop in range(1, SIDE):
        seat_to = seat_after(hop)
        parts.append(
            copy(
                sent_ref.at[rows_of(seat_to)], part_ref.at[hop - 1],
                part_send.at[hop - 1], part_recv.at[hop - 1], device(plane, seat_to),
            )
        )
        parts[-1].start()
    held = [sent_ref[rows_of(seat)].astype(jnp.float32)]
    for hop in range(1, SIDE):
        parts[hop - 1].wait_recv()
        held.append(part_ref[hop - 1].astype(jnp.float32))
    total_ref[...] = functools.reduce(jnp.add, held).astype(jnp.bfloat16)
    planes = [
        copy(
            total_ref, plane_ref.at[hop - 1], plane_send.at[hop - 1], plane_recv.at[hop - 1],
            device((plane + hop) % SIDE, seat),
        )
        for hop in range(1, SIDE)
    ]
    for hop in range(1, SIDE):
        pl.when(plane + hop < SIDE)(planes[hop - 1].start)

    def earlier_seats(limit):
        total = jnp.zeros_like(held[0])
        for hop in range(SIDE):
            total = total + jnp.where((seat + SIDE - hop) % SIDE < limit, held[hop], 0.0)
        return total

    early_ref[...] = jnp.zeros_like(early_ref)
    for hop in range(1, SIDE):

        @pl.when(plane >= hop)
        def _(hop=hop):
            planes[hop - 1].wait_recv()
            early_ref[...] += plane_ref[hop - 1].astype(jnp.float32)

    early = early_ref[...]
    stages = []
    for hop in range(1, SIDE):
        seat_to = seat_after(hop)
        stage_ref[hop - 1] = early + earlier_seats(seat_to)
        stages.append(
            copy(
                stage_ref.at[hop - 1], before_ref.at[rows_of(seat)],
                stage_send.at[hop - 1], stage_recv.at[hop - 1], device(plane, seat_to),
            )
        )
        stages[-1].start()
    own_rows = rows_of(seat)

    def settle(rows, before):
        if last:
            out_ref[rows] = before + increment_ref[rows]
        else:
            out_ref[rows] = jnp.where(timestep == 0, latent_ref[rows], before)

    settle(own_rows, early + earlier_seats(seat))
    for hop in range(1, SIDE):
        stages[hop - 1].wait_recv()
        rows = rows_of((seat + SIDE - hop) % SIDE)
        settle(rows, before_ref[rows])
    for hop in range(1, SIDE):
        parts[hop - 1].wait_send()
        pl.when(plane + hop < SIDE)(planes[hop - 1].wait_send)
        stages[hop - 1].wait_send()


def carried_kernel(last, groups, sent, increment, latent):
    rows, lanes = sent.shape
    quarter = rows // SIDE
    hops = SIDE - 1
    vmem = pl.BlockSpec(memory_space=pltpu.VMEM)
    return pl.pallas_call(
        functools.partial(carry_kernel, last, groups),
        out_shape=jax.ShapeDtypeStruct((rows, lanes), jnp.float32),
        in_specs=[vmem] * 3,
        out_specs=vmem,
        scratch_shapes=[
            pltpu.VMEM((hops, quarter, lanes), jnp.bfloat16),
            pltpu.VMEM((quarter, lanes), jnp.bfloat16),
            pltpu.VMEM((hops, quarter, lanes), jnp.bfloat16),
            pltpu.VMEM((quarter, lanes), jnp.float32),
            pltpu.VMEM((hops, quarter, lanes), jnp.float32),
            pltpu.VMEM((rows, lanes), jnp.float32),
        ]
        + [pltpu.SemaphoreType.DMA((hops,))] * 6,
        compiler_params=pltpu.CompilerParams(collective_id=int(last), has_side_effects=True),
        name="carry_last" if last else "carry",
    )(sent, increment, latent)


def carried_in(last, groups, same_block, timestep, sent, increment, latent):
    rows = sent.size // LANES
    if sent.shape[-1] == LANES and rows % (SIDE * 16) == 0:
        flat = [array.reshape(rows, LANES) for array in (sent, increment, latent)]
        return carried_kernel(last, groups, *flat).reshape(latent.shape)
    gathered = lax.all_gather(
        sent, "tok", axis_index_groups=same_block if groups > 1 else None
    )
    earlier = (jnp.arange(P_SIZE) < timestep)[:, None, None, None]
    before = jnp.sum(jnp.where(earlier, gathered.astype(jnp.float32), 0.0), axis=0)
    return before + increment if last else jnp.where(timestep == 0, latent, before)


def body(
    initial_guess,
    noise_draws,
    drift_state,
    drift_denoise,
    noise_scale,
    modulation,
    embed_weight,
    space_input,
    space_output,
    time_input,
    time_output,
    final_weight,
):
    devices = lax.axis_size("tok")
    own_index = lax.axis_index("tok")
    groups = devices // P_SIZE
    timestep = own_index // groups
    own = jnp.reshape(timestep, (1,)).astype(jnp.int32)
    rates = (drift_state, drift_denoise, noise_scale)
    same_step = [[step * groups + block for block in range(groups)] for step in range(P_SIZE)]
    same_block = [[step * groups + block for step in range(P_SIZE)] for block in range(groups)]
    first, offset, packed, square, shift = fold(
        own, modulation, embed_weight, space_input.T, space_output, time_input.T, time_output,
        final_weight.T,
    )
    latent = initial_guess
    for iteration in range(ITERS):
        tokens = space_block(latent, first, offset)
        if groups == 1:
            increment, sent = time_block(
                own, tokens, packed, square, shift, (latent, noise_draws) + rates
            )
        else:
            tokens = lax.all_to_all(
                tokens, "tok", split_axis=1, concat_axis=0, axis_index_groups=same_step, tiled=True
            )
            (predicted,) = time_block(own, tokens, packed, square, shift)
            predicted = lax.all_to_all(
                predicted, "tok", split_axis=0, concat_axis=2, axis_index_groups=same_step, tiled=True
            )
            rate_state, rate_denoise, rate_noise = (
                lax.dynamic_index_in_dim(rate, timestep, 0, keepdims=False) for rate in rates
            )
            rate_state = rate_state + jnp.where(timestep == 0, 1.0, 0.0)
            increment = rate_state * latent + rate_denoise * predicted + rate_noise * noise_draws
            sent = increment.astype(jnp.bfloat16)
        latent = carried_in(
            iteration == ITERS - 1, groups, same_block, timestep, sent, increment, latent
        )
    return latent


def solution(mesh):
    placed = (
        P(("group", "tok"), None, None),
        P(("group", "tok"), None, None),
        P(),
        P(),
        P(),
        P(),
        P(),
        P(),
        P(),
        P(),
        P(),
        P(),
    )
    return jax.shard_map(
        body, mesh=mesh, in_specs=placed, out_specs=P(("group", "tok"), None, None), check_vma=False
    )
```

time: 157 us -> 100 us (0.64)
  Pallas kernels: 154 us -> 97.3 us
    pallas_call x2, Pallas kernels: 58.1 us -> 20.3 us  [space_block(): pl.pallas_call(space_kernel, out_shape=jax.ShapeDtypeStruct((frames, spat...]
    pallas_call x2, Pallas kernels: 70 us -> 39.5 us  [time_block(): pl.pallas_call(functools.partial(time_kernel, bool(fused)), out_shape=[ja...]
    pallas_call x0 -> x1, Pallas kernels: none -> 11.6 us  [fold(): pl.pallas_call(fold_kernel, out_shape=[jax.ShapeDtypeStruct(*shape) for s...]
where the time goes in v1:
time: 100 us; the launch traced here: 98.9 us
  Pallas kernels  97.3 us (97%)
  local copies, waits for them, and re-layouts  1.57 us (2%)
    pallas_call x2, Pallas kernels, time_block(): pl.pallas_call(functools.partial(time_kernel, bool(fused)), out_shape=[ja...  39.5 us
    pallas_call x2, Pallas kernels, carried_kernel(): pl.pallas_call(functools.partial(carry_kernel, last, groups), out_shape=j...  26 us
    pallas_call x2, Pallas kernels, space_block(): pl.pallas_call(space_kernel, out_shape=jax.ShapeDtypeStruct((frames, spat...  20.3 us
    pallas_call x1, Pallas kernels, fold(): pl.pallas_call(fold_kernel, out_shape=[jax.ShapeDtypeStruct(*shape) for s...  11.6 us

profile of v1, /device:TPU:0, one launch (start us, length us, event | category | flops | bytes accessed | tf_op | source)
XLA Modules:
  0.0 98.9 jit_solution(3862605663610408171)
XLA Ops:
  0.0 11.6 %fold.1 = (bf16[416,32]{1,0:T(8,128)(2,1)}, f32[408,128]{1,0:T(8,128)}, bf16[256,2688]{1,0:T(8,128)(2,1)}, bf16[768,768]{1,0:T(8,128)(2,1)}, f32[16,128]{1,0:T(8,128)}) custom-call(s32[1]{0:T(128)} %bitcast.step_ref.refs_0_, f32[16,8,1152]{2,1,0:T(8,128)} %table_ref.1, bf16[16,1152]{1,0:T(8,128)(2,1)} %embed_ref.1, bf16[1728,1152]{1,0:T(8,128)(2,1)} %bitcast.11, ...), custom_call_target="tpu_custom_call" | custom-call | tf_op jit(solution)/shard_map/fold/pallas_call | solution.py:450
  11.6 10.1 %space_block.2.refs_1_ = bf16[16,128,256]{2,1,0:T(8,128)(2,1)} custom-call(f32[16,16,128]{2,1,0:T(8,128)} %refs_5_.1, bf16[416,32]{1,0:T(8,128)(2,1)} %get-tuple-element.14.first_ref, f32[408,128]{1,0:T(8,128)} %get-tuple-element.15.offset_ref), custom_call_target="tpu_custom_call" | custom-call | tf_op jit(solution)/shard_map/space_block/pallas_call | solution.py:478
  21.7 19.7 %time_block.2 = (f32[16,16,128]{2,1,0:T(8,128)}, bf16[16,16,128]{2,1,0:T(8,128)(2,1)}) custom-call(s32[1]{0:T(128)} %bitcast.step_ref.refs_0_, bf16[16,128,256]{2,1,0:T(8,128)(2,1)} %space_block.2.refs_1_, bf16[256,2688]{1,0:T(8,128)(2,1)} %get-tuple-element.16.refs_2_, bf16[768,768]{1,0:T(8,128)(2,1)} %get-tuple-element.17.refs_3_, ...), custom_call_target="tpu_custom_call" | custom-call | tf_op jit(solution)/shard_map/time_block/pallas_call | solution.py:498
  41.4 12.7 %carry.1.latent_ref = f32[256,128]{1,0:T(8,128)} custom-call(bf16[256,128]{1,0:T(8,128)(2,1)} %bitcast.20, f32[256,128]{1,0:T(8,128)} %bitcast.18, f32[256,128]{1,0:T(8,128)} %bitcast.15), custom_call_target="tpu_custom_call" | custom-call | tf_op jit(solution)/shard_map/carry/pallas_call | solution.py:637
  54.1 10.1 %space_block.3.refs_1_ = bf16[16,128,256]{2,1,0:T(8,128)(2,1)} custom-call(f32[16,16,128]{2,1,0:T(8,128)} %bitcast.13, bf16[416,32]{1,0:T(8,128)(2,1)} %get-tuple-element.14.first_ref, f32[408,128]{1,0:T(8,128)} %get-tuple-element.15.offset_ref), custom_call_target="tpu_custom_call" | custom-call | tf_op jit(solution)/shard_map/space_block/pallas_call | solution.py:478
  64.3 19.7 %time_block.3 = (f32[16,16,128]{2,1,0:T(8,128)}, bf16[16,16,128]{2,1,0:T(8,128)(2,1)}) custom-call(s32[1]{0:T(128)} %bitcast.step_ref.refs_0_, bf16[16,128,256]{2,1,0:T(8,128)(2,1)} %space_block.3.refs_1_, bf16[256,2688]{1,0:T(8,128)(2,1)} %get-tuple-element.16.refs_2_, bf16[768,768]{1,0:T(8,128)(2,1)} %get-tuple-element.17.refs_3_, ...), custom_call_target="tpu_custom_call" | custom-call | tf_op jit(solution)/shard_map/time_block/pallas_call | solution.py:498
  84.0 13.3 %carry_last.1 = f32[256,128]{1,0:T(8,128)} custom-call(bf16[256,128]{1,0:T(8,128)(2,1)} %bitcast.19, f32[256,128]{1,0:T(8,128)} %bitcast.17, f32[256,128]{1,0:T(8,128)} %carry.1.latent_ref), custom_call_target="tpu_custom_call" | custom-call | tf_op jit(solution)/shard_map/carry_last/pallas_call | solution.py:637
  97.4 1.6 %copy.14 = f32[16,16,128]{2,1,0:T(8,128)} copy(f32[16,16,128]{2,1,0:T(8,128)} %bitcast.16) | data formatting | bytes 262144

commit v2 on v1

--- a/solution.py
+++ b/solution.py
@@ -22,8 +22,6 @@
 ROWS_AA = 3 * ROWS_T + 32
 BASE = 512
 TAIL = INNER - BASE
-V_COLS = BASE + LANES
-PACKED = 2 * HEADS * LANES + V_COLS
 LAT, DUP, ZERO, ONE, ATT = 128, 144, 160, 184, 192
 SCALE = HD**-0.5 * math.log2(math.e)
 UNIT = HD**0.5 * math.log2(math.e)
@@ -173,17 +171,9 @@
             axis=0,
         ).astype(jnp.bfloat16)
 
-    packed_ref[...] = jnp.zeros_like(packed_ref)
     for which in range(3):
-        columns = settle(dot_rows(rows, time_in_ref[which * INNER : (which + 1) * INNER, :]))
-        if which == 2:
-            start = 2 * HEADS * LANES
-            packed_ref[:, start : start + BASE] = columns[:, :BASE]
-            packed_ref[:, start + BASE + LANES - TAIL : start + V_COLS] = columns[:, BASE:]
-        else:
-            for head in range(HEADS):
-                start = (which * HEADS + head) * LANES
-                packed_ref[:, start : start + HD] = columns[:, head * HD : (head + 1) * HD]
+        own = slice(which * INNER, (which + 1) * INNER)
+        packed_ref[own] = settle(dot_rows(rows, time_in_ref[own, :])).T
 
     gate = table(5)
     lat_high, lat_low = halves(embed)
@@ -215,44 +205,83 @@
         ],
         axis=0,
     )
-    lane = lane_of((1, WIDE))
-    plain = (lane >= ZERO) & (lane < ZERO + CHANNELS)
+    line = row_of((WIDE, 1))
+    plain = (line >= ZERO) & (line < ZERO + CHANNELS)
     tiles = lines_ref.shape[0] // WIDE
     for column in range(tiles):
         other = lines_ref[column * WIDE : (column + 1) * WIDE] if column else base
         for row in range(column, tiles):
-            block = dot_rows(lines_ref[row * WIDE : (row + 1) * WIDE], other)
+            block = dot_rows(other, lines_ref[row * WIDE : (row + 1) * WIDE])
             block = block * ((1.0 if row == column else 2.0) / features) if column else (
                 block * jnp.where(plain, 1.0, (1.0 if row == column else 2.0) / features)
             )
-            square_ref[row * WIDE : (row + 1) * WIDE, column * WIDE : (column + 1) * WIDE] = (
+            square_ref[column * WIDE : (column + 1) * WIDE, row * WIDE : (row + 1) * WIDE] = (
                 block.astype(jnp.bfloat16)
             )
 
 
-def space_kernel(latent_ref, first_ref, offset_ref, token_ref):
+def stack(*parts):
+    return jnp.concatenate(parts, axis=0)
+
+
+def beside(*parts):
+    return jnp.concatenate(parts, axis=1)
+
+
+def on_diagonal(first, second):
+    blank = jnp.zeros_like(first)
+    return stack(beside(first, blank), beside(blank, second))
+
+
+def interleave(tasks):
+    tasks, running = list(tasks), []
+    while tasks or running:
+        running += [tasks.pop(0)] if tasks else []
+        running = [task for task in running if next(task, tasks) is not tasks]
+
+
+def pause(turns):
+    for turn in range(turns):
+        yield
+
+
+def wait_for(state, key):
+    while key not in state:
+        yield
+
+
+def space_kernel(lags, latent_ref, first_ref, offset_ref, token_ref):
     frames, channels, spatial = latent_ref.shape
     bf16 = jnp.bfloat16
     f32 = jnp.float32
-    head_lane = lane_of((spatial, LANES)) // CHANNELS
-    head_row = row_of((HEADS, spatial))
-    kept = lane_of((spatial, 64))
-    kept = (kept < 32) | (kept >= 56)
+    row = row_of((8, spatial))
+    blank = jnp.zeros((8, spatial), f32)
+    ones = jnp.ones((8, spatial), f32)
+    states = [{} for frame in range(frames)]
 
     def offset(start, rows):
         return offset_ref[start : start + rows]
 
-    stacked = []
-    for frame in range(frames):
+    def twice(frame):
         latent = latent_ref[frame].astype(bf16)
-        stacked.append(jnp.concatenate([latent, latent], axis=0))
-    product = dot(first_ref[...], jnp.concatenate(stacked, axis=1))
-    for frame in range(frames):
-        result = product[:, frame * spatial : (frame + 1) * spatial]
-        latent = stacked[frame][:channels].astype(f32)
+        return stack(latent, latent)
+
+    def couple_task(frame):
+        own = range(frame, min(frame + 2, frames))
+        product = dot(first_ref[...], beside(*(twice(index) for index in own)))
+        yield from pause(lags[0])
+        for place, index in enumerate(own):
+            states[index]["result"] = product[:, place * spatial : (place + 1) * spatial]
+
+    def frame_task(frame):
+        state = states[frame]
+        yield from wait_for(state, "result")
+        result = state["result"]
+        latent = latent_ref[frame].astype(bf16).astype(f32)
         gram = result[3 * ROWS_T + 8 : 3 * ROWS_T + 8 + channels]
         variance = jnp.maximum(jnp.sum(latent * gram, 0, keepdims=True), 0.0) + EPS
         rate = lax.rsqrt(variance)
+        yield
         spread = variance * rate
         scaled = latent * rate
 
@@ -264,58 +293,68 @@
             total = jnp.sum(terms, 0) + offset(place + ROWS_T, 8)
             return lax.rsqrt(jnp.maximum(total, 0.0) + EPS)
 
-        key_rate, query_rate = norm(0), norm(1)
-        query_rate = (query_rate * rate).T
-        terms = rate * result[:ROWS_T] + offset(0, ROWS_T)
+        key_rate = norm(0)
+        yield
+        query_rate = norm(1) * rate
+        yield
         point = (rate * result[ROWS_T : ROWS_T + 8] + offset(ROWS_T, 8)) * key_rate
         point_high = point.astype(bf16).astype(f32)
-        point_low = point - point_high
-        spread = jnp.broadcast_to(spread, (8, spatial))
         spread_high = spread.astype(bf16).astype(f32)
-        ends = jnp.concatenate(
-            [spread_high, spread - spread_high, spread_high, jnp.ones_like(spread)], axis=0
-        ).astype(bf16)
-        tokens = jnp.concatenate([stacked[frame], ends], axis=0).T
-
-        def columns(head):
-            own = terms[head * channels : (head + 1) * channels] * key_rate[head : head + 1]
-            high, low = halves(own)
-            mine = head_row == head
-            point_mine = jnp.where(mine, point_high, 0.0)
-            ends = jnp.concatenate(
-                [point_mine, point_mine, jnp.where(mine, point_low, 0.0), jnp.zeros_like(point_mine)],
-                axis=0,
-            ).astype(bf16)
-            return jnp.concatenate([high, low, ends], axis=0)
-
-        spot = jnp.concatenate([scaled] * HEADS, axis=0).astype(bf16).T
-        mixed = None
-        weights, sources = [], []
-        for pair in range(HEADS // 2):
-            heads = (2 * pair, 2 * pair + 1)
-            score = dot(tokens, jnp.concatenate([columns(head) for head in heads], axis=1))
-            for place, head in enumerate(heads):
-                own = score[:, place * spatial : (place + 1) * spatial]
-                weights.append(jnp.exp2(own * query_rate[:, head : head + 1]).astype(bf16))
-                mine = head_lane == head
-                sources.append(
-                    jnp.concatenate(
-                        [
-                            jnp.where(mine, spot, jnp.zeros_like(spot)),
-                            jnp.where(mine, 1.0, 0.0).astype(bf16),
-                        ],
-                        axis=1,
-                    )
-                )
-        mixed = dot(jnp.concatenate(weights, axis=1), jnp.concatenate(sources, axis=0))
-        average = mixed[:, :LANES] / mixed[:, LANES:]
-        token_ref[frame, :, :LANES] = average.astype(bf16)
-        token_ref[frame, :, LANES:] = jnp.concatenate(
-            [jnp.where(kept, tokens, jnp.zeros_like(tokens)), jnp.zeros_like(tokens)], axis=1
-        )
-
-
-def time_kernel(fused, *refs):
+        ends = jnp.where(row == 1, spread - spread_high, jnp.where(row < 3, spread_high, 0.0))
+        source = stack(twice(frame), stack(ends, blank).astype(bf16))
+        state.update(
+            terms=lambda start: rate * result[start : start + channels] + offset(start, channels),
+            key_rate=key_rate,
+            query_rate=query_rate,
+            point=(point_high, point - point_high),
+            right=on_diagonal(source, source),
+            rows=stack(scaled, ones, blank).astype(bf16),
+            averages=[],
+        )
+
+    def pair_task(frame, pair):
+        state = states[frame]
+        heads = (2 * pair, 2 * pair + 1)
+        yield from wait_for(state, "rows")
+        left = []
+        for head in heads:
+            own = state["terms"](head * channels) * state["key_rate"][head : head + 1]
+            high, low = (part[head : head + 1] for part in state["point"])
+            own_point = jnp.where(row < 2, high, jnp.where(row == 2, low, 0.0))
+            left += [*halves(own), stack(own_point, blank).astype(bf16)]
+        left = stack(*left).T
+        yield
+        score = dot(left, state["right"])
+        yield from pause(lags[1])
+        pace = beside(*(state["query_rate"][head : head + 1] for head in heads))
+        weight = jnp.exp2(score * pace).astype(bf16)
+        yield
+        mixed = dot(state["rows"], weight)
+        yield from pause(lags[2])
+        share = 1.0 / mixed[channels : channels + 8]
+        mixed = (mixed[:channels].reshape(-1, 8, 2 * spatial) * share[None]).reshape(channels, -1)
+        state["averages"] += [mixed[:, :spatial], mixed[:, spatial:]]
+        if pair == HEADS // 2 - 1:
+            latent = latent_ref[frame].astype(bf16).astype(f32)
+            token = stack(
+                *state["averages"], latent, latent, blank, blank, blank, ones, *[blank] * 8
+            )
+            token_ref[frame] = token.astype(bf16).T
+
+    def tasks():
+        for frame in range(-2, frames):
+            ahead = frame + 2
+            if ahead < frames:
+                if ahead % 2 == 0:
+                    yield couple_task(ahead)
+                yield frame_task(ahead)
+            if frame >= 0:
+                yield from (pair_task(frame, pair) for pair in range(HEADS // 2))
+
+    interleave(tasks())
+
+
+def time_kernel(lags, fused, *refs):
     step_ref, token_ref, packed_ref, square_ref, shift_ref, *refs = refs
     if fused:
         latent_ref, noise_ref, *rate_refs, increment_ref, sent_ref = refs[:7]
@@ -325,91 +364,114 @@
     bf16 = jnp.bfloat16
     f32 = jnp.float32
     frames, positions, width = token_ref.shape
-    count = frames * positions
     chunk = 8
     rows = frames * chunk
-    tokens = token_ref[...].reshape(count, width)
-    variance = jnp.sum(tokens.astype(f32) * dot(tokens, square_ref[:WIDE, :WIDE]), -1, keepdims=True)
-    variance = jnp.maximum(variance, 0.0) + EPS
-    pace = lax.rsqrt(variance)
-    spread = variance * pace
-    spread_high = spread.astype(bf16).astype(f32)
-    lane = lane_of((count, LANES))
-    upper = tokens[:, LANES:].astype(f32)
-    upper = jnp.where((lane == ZERO - LANES) | (lane == ZERO - LANES + 2), spread_high, upper)
-    upper = jnp.where(lane == ZERO - LANES + 1, spread - spread_high, upper)
-    entry = jnp.concatenate([tokens[:, :LANES], upper.astype(bf16)], axis=1)
-    packed = dot(entry, packed_ref[...])
-    floor = (HD * EPS) * variance
-    keep = (row_of((rows, rows)) % chunk) == (lane_of((rows, rows)) % chunk)
-    value_lane = lane_of((rows, V_COLS))
-    value_lane = jnp.where(value_lane < BASE, value_lane, jnp.where(value_lane < BASE + LANES - TAIL, -1, value_lane - (LANES - TAIL)))
-    value_head = jnp.where(value_lane < 0, -1, value_lane // HD)
-    parts = positions // chunk
-
-    def of_part(values, part):
-        lanes = values.shape[1]
-        return values.reshape(frames, parts, chunk, lanes)[:, part].reshape(rows, lanes)
-
-    for part in range(parts):
-        own_floor = of_part(floor, part)
-        own_tokens = of_part(tokens.astype(f32), part)
-        values = of_part(packed[:, 2 * HEADS * LANES :], part) * of_part(pace, part)
-        values = values.astype(bf16)
-
-        def slab(which, head, gain):
-            start = (which * HEADS + head) * LANES
-            own = of_part(packed[:, start : start + LANES], part)
-            size = lax.rsqrt(jnp.sum(own * own, -1, keepdims=True) + own_floor)
-            return (own * (size * gain if gain else size)).astype(bf16)
-
-        weights = []
-        for pair in range(HEADS // 2):
-            heads = (2 * pair, 2 * pair + 1)
-            query = jnp.concatenate([slab(0, head, UNIT) for head in heads], axis=1)
-            key = [slab(1, head, None) for head in heads]
-            blank = jnp.zeros_like(key[0])
-            keys = jnp.concatenate(
-                [jnp.concatenate([key[0], blank], axis=1), jnp.concatenate([blank, key[1]], axis=1)],
-                axis=0,
-            )
-            score = dot_rows(query, keys)
-            for place in range(2):
-                weight = jnp.where(keep, jnp.exp2(score[:, place * rows : (place + 1) * rows]), 0.0)
-                total = jnp.sum(weight, -1, keepdims=True)
-                weights.append((weight * (1.0 / total)).astype(bf16))
-
-        def mixed(heads, start, stop):
-            source = [
-                jnp.where(value_head[:, start:stop] == head, values[:, start:stop], jnp.zeros((), bf16))
-                for head in heads
-            ]
-            return dot(
-                jnp.concatenate([weights[head] for head in heads], axis=1),
-                jnp.concatenate(source, axis=0),
-            )
-
-        def heads_in(start, stop):
-            return range(start // HD, (stop - 1) // HD + 1)
-
-        low = mixed(heads_in(0, WIDE), 0, WIDE)
-        high = mixed(heads_in(WIDE, BASE), WIDE, BASE)
-        tail = mixed(heads_in(BASE, INNER), BASE, V_COLS)
-        state = jnp.concatenate(
-            [own_tokens[:, :LANES], own_tokens[:, LANES:] + tail, low, high], axis=1
-        ).astype(bf16)
-        total = jnp.zeros((rows, LANES), f32)
-        for column in range(state.shape[1] // WIDE):
-            own = slice(column * WIDE, (column + 1) * WIDE)
-            block = dot(state[:, column * WIDE :], square_ref[column * WIDE :, own])
-            if column == 0:
-                predicted = block[:, LANES:]
-            for half in range(2):
-                lanes = slice(half * LANES, (half + 1) * LANES)
-                total = total + block[:, lanes] * state[:, own][:, lanes].astype(f32)
-        rate = lax.rsqrt(jnp.maximum(jnp.sum(total, -1, keepdims=True), 0.0) + EPS)
-        start = pl.multiple_of(pl.program_id(0) * positions + part * chunk, chunk)
-        predicted_ref[:, pl.ds(start, chunk), :] = (predicted * rate).reshape(frames, chunk, LANES)
+    size = math.gcd(positions, 2 * chunk)
+    parts = size // chunk
+    groups = positions // size
+    count = parts * rows
+    keep = (row_of((rows, 2 * rows)) % chunk) == (lane_of((rows, 2 * rows)) % chunk)
+    ones = jnp.ones((8, rows), f32)
+    row = row_of((16, count))
+    states = [{} for group in range(groups)]
+
+    def group_task(group):
+        state = states[group]
+        tokens = token_ref[:, group * size : (group + 1) * size, :].astype(f32)
+        tokens = tokens.reshape(frames, parts, chunk, width)
+        tokens = beside(
+            *(tokens[:, part].reshape(rows, width).astype(bf16).T for part in range(parts))
+        )
+        yield
+        squares = dot(square_ref[:ATT, :WIDE], tokens)
+        yield from pause(lags[0])
+        variance = jnp.sum(tokens[:ATT].astype(f32) * squares, 0, keepdims=True)
+        variance = jnp.maximum(variance, 0.0) + EPS
+        pace = lax.rsqrt(variance)
+        spread = variance * pace
+        spread_high = spread.astype(bf16).astype(f32)
+        yield
+        ends = jnp.where(row == 1, spread - spread_high, jnp.where(row < 3, spread_high, 0.0))
+        state.update(
+            tokens=tokens, pace=pace, floor=(HD * EPS) * variance, outputs={},
+            entry=stack(tokens[:ZERO], ends.astype(bf16), tokens[ZERO + 16 :]),
+        )
+
+    def project_task(group, pair):
+        state = states[group]
+        yield from wait_for(state, "entry")
+        starts = [which * INNER + pair * 2 * HD for which in range(3)]
+        packed = [dot(packed_ref[start : start + 2 * HD], state["entry"]) for start in starts]
+        yield from pause(lags[1])
+        state["packed", pair] = packed
+
+    def pair_task(group, pair, part):
+        state = states[group]
+        own = slice(part * rows, (part + 1) * rows)
+        yield from wait_for(state, ("packed", pair))
+        packed = [values[:, own] for values in state["packed", pair]]
+
+        def unit(which, head, gain):
+            values = packed[which][head * HD : (head + 1) * HD]
+            size = lax.rsqrt(jnp.sum(values * values, 0, keepdims=True) + state["floor"][:, own])
+            return values * (size * gain if gain else size)
+
+        left = stack(unit(1, 0, None), unit(1, 1, None), jnp.zeros((16, rows), f32)).astype(bf16).T
+        yield
+        right = on_diagonal(unit(0, 0, UNIT), unit(0, 1, UNIT))
+        right = stack(right, jnp.zeros((16, 2 * rows), f32)).astype(bf16)
+        score = dot(left, right)
+        yield from pause(lags[2])
+        weight = jnp.where(keep, jnp.exp2(score), 0.0).astype(bf16)
+        yield
+        value = packed[2] * state["pace"][:, own]
+        value = beside(stack(value[:HD], ones), stack(value[HD:], ones)).astype(bf16)
+        mixed = dot(value, on_diagonal(weight[:, :rows], weight[:, rows:]))
+        yield from pause(lags[3])
+        share = 1.0 / mixed[HD:]
+        mixed = (mixed[:HD].reshape(-1, 8, 2 * rows) * share[None]).reshape(HD, 2 * rows)
+        state["outputs"][part, pair] = stack(mixed[:, :rows], mixed[:, rows:])
+
+    def last_task(group):
+        state = states[group]
+        while len(state.get("outputs", ())) < parts * HEADS // 2:
+            yield
+        attended = beside(
+            *(
+                stack(*(state["outputs"][part, pair] for pair in range(HEADS // 2)))
+                for part in range(parts)
+            )
+        )
+        exact = stack(state["tokens"][:ATT].astype(f32), attended[BASE:], attended[:BASE])
+        inputs = exact.astype(bf16)
+        yield
+        blocks = []
+        for start in range(0, exact.shape[0], WIDE):
+            blocks.append(dot(square_ref[start : start + WIDE, start:], inputs[start:]))
+            yield
+        yield from pause(lags[4])
+        total = 0.0
+        for index, block in enumerate(blocks):
+            terms = block * exact[index * WIDE : (index + 1) * WIDE]
+            total = total + jnp.sum(terms.reshape(-1, 8, count), 0)
+        rate = lax.rsqrt(jnp.maximum(jnp.sum(total, 0, keepdims=True), 0.0) + EPS)
+        yield
+        predicted = blocks[0][ZERO : ZERO + CHANNELS] * rate
+        for part in range(parts):
+            index = (pl.program_id(0) * groups + group) * parts + part
+            predicted_ref[index] = predicted[:, part * rows : (part + 1) * rows]
+
+    def tasks():
+        yield group_task(0)
+        for group in range(groups):
+            for pair in range(HEADS // 2):
+                yield project_task(group, pair)
+                if pair == 1 and group + 1 < groups:
+                    yield group_task(group + 1)
+                yield from (pair_task(group, pair, part) for part in range(parts))
+            yield last_task(group)
+
+    interleave(tasks())
 
     @pl.when(pl.program_id(0) == pl.num_programs(0) - 1)
     def _():
@@ -417,8 +479,26 @@
             timestep = step_ref[0]
             rate_state, rate_denoise, rate_noise = (ref[timestep] for ref in rate_refs)
             rate_state = rate_state + jnp.where(timestep == 0, 1.0, 0.0)
+        chunks = [predicted_ref[index] for index in range(predicted_ref.shape[0])]
+        block = lane_of(chunks[0].shape) // chunk
+        if len(chunks) == frames and frames & (frames - 1) == 0:
+            step = 1
+            while step < frames:
+                moved = (block & step) != 0
+                for low in range(frames):
+                    if low & step == 0:
+                        first, second = chunks[low], chunks[low + step]
+                        chunks[low] = jnp.where(moved, pltpu.roll(second, step * chunk, 1), first)
+                        chunks[low + step] = jnp.where(
+                            moved, second, pltpu.roll(first, rows - step * chunk, 1)
+                        )
+                step *= 2
+            turned_of = chunks.__getitem__
+        else:
+            def turned_of(frame):
+                return beside(*(part[:, frame * chunk : (frame + 1) * chunk] for part in chunks))
         for frame in range(frames):
-            turned = predicted_ref[frame].T[ZERO - LANES : ZERO - LANES + CHANNELS]
+            turned = turned_of(frame)
             turned = turned + shift_ref[:, : turned.shape[1]]
             if fused:
                 turned = (
@@ -442,7 +522,7 @@
     shapes = [
         ((ROWS_AA, 2 * CHANNELS), jnp.bfloat16),
         ((3 * (ROWS_T + 8), LANES), jnp.float32),
-        ((WIDE, PACKED), jnp.bfloat16),
+        ((3 * INNER, WIDE), jnp.bfloat16),
         ((BASE + WIDE, BASE + WIDE), jnp.bfloat16),
         ((CHANNELS, LANES), jnp.float32),
     ]
@@ -474,9 +554,9 @@
 
 def space_block(latent, first, offset):
     frames, channels, spatial = latent.shape
-    step_frames = math.gcd(frames, 2)
+    step_frames = math.gcd(frames, 16)
     return pl.pallas_call(
-        space_kernel,
+        functools.partial(space_kernel, (2, 3, 2)),
         out_shape=jax.ShapeDtypeStruct((frames, spatial, WIDE), jnp.bfloat16),
         grid=(frames // step_frames,),
         in_specs=[
@@ -492,11 +572,11 @@
 
 def time_block(own, tokens, packed, square, shift, fused=()):
     frames, positions, width = tokens.shape
-    step_positions = math.gcd(positions, 16)
+    step_positions = math.gcd(positions, 64)
     shape = (frames, CHANNELS, positions)
     kinds = [jnp.float32] + [jnp.bfloat16] * bool(fused)
     return pl.pallas_call(
-        functools.partial(time_kernel, bool(fused)),
+        functools.partial(time_kernel, (2, 2, 3, 2, 1), bool(fused)),
         out_shape=[jax.ShapeDtypeStruct(shape, kind) for kind in kinds],
         grid_spec=pltpu.PrefetchScalarGridSpec(
             num_scalar_prefetch=1,
@@ -515,7 +595,7 @@
                 pl.BlockSpec(shape, lambda step, own: (0, 0, 0), pipeline_mode=pl.Buffered(1))
                 for kind in kinds
             ],
-            scratch_shapes=[pltpu.VMEM((frames, positions, LANES), jnp.float32)],
+            scratch_shapes=[pltpu.VMEM((positions // 8, CHANNELS, frames * 8), jnp.float32)],
         ),
         compiler_params=pltpu.CompilerParams(vmem_limit_bytes=60 * 1024 * 1024),
         name="time_block",

time: 100 us -> 82.7 us (0.83)
  Pallas kernels: 97.3 us -> 79.9 us
    pallas_call x4, Pallas kernels: 59.7 us -> 42.4 us  [the longest x2 30 us: time_block(): pl.pallas_call(functools.partial(time_kernel, (2, 2, 3, 2, 1), bool(fused...]
where the time goes in v2:
time: 82.7 us; the launch traced here: 81.4 us
  Pallas kernels  79.9 us (97%)
  local copies, waits for them, and re-layouts  1.57 us (2%)
    pallas_call x2, Pallas kernels, time_block(): pl.pallas_call(functools.partial(time_kernel, (2, 2, 3, 2, 1), bool(fused...  30 us
    pallas_call x2, Pallas kernels, carried_kernel(): pl.pallas_call(functools.partial(carry_kernel, last, groups), out_shape=j...  26.1 us
    pallas_call x2, Pallas kernels, space_block(): pl.pallas_call(functools.partial(space_kernel, (2, 3, 2)), out_shape=jax....  12.4 us
    pallas_call x1, Pallas kernels, fold(): pl.pallas_call(fold_kernel, out_shape=[jax.ShapeDtypeStruct(*shape) for s...  11.4 us

profile of v2, /device:TPU:0, one launch (start us, length us, event | category | flops | bytes accessed | tf_op | source)
XLA Modules:
  0.0 81.4 jit_solution(15594642357225859312)
XLA Ops:
  0.0 11.4 %fold.1 = (bf16[416,32]{1,0:T(8,128)(2,1)}, f32[408,128]{1,0:T(8,128)}, bf16[1728,256]{1,0:T(8,128)(2,1)}, bf16[768,768]{1,0:T(8,128)(2,1)}, f32[16,128]{1,0:T(8,128)}) custom-call(s32[1]{0:T(128)} %bitcast.step_ref.refs_0_, f32[16,8,1152]{2,1,0:T(8,128)} %table_ref.1, bf16[16,1152]{1,0:T(8,128)(2,1)} %embed_ref.1, bf16[1728,1152]{1,0:T(8,128)(2,1)} %bitcast.11, ...), custom_call_target="tpu_custom_call" | custom-call | tf_op jit(solution)/shard_map/fold/pallas_call | solution.py:530
  11.4 6.2 %space_block.2.refs_1_ = bf16[16,128,256]{2,1,0:T(8,128)(2,1)} custom-call(f32[16,16,128]{2,1,0:T(8,128)} %refs_5_.1, bf16[416,32]{1,0:T(8,128)(2,1)} %get-tuple-element.14.first_ref, f32[408,128]{1,0:T(8,128)} %get-tuple-element.15.offset_ref), custom_call_target="tpu_custom_call" | custom-call | tf_op jit(solution)/shard_map/space_block/pallas_call | solution.py:558
  17.6 15.0 %time_block.2 = (f32[16,16,128]{2,1,0:T(8,128)}, bf16[16,16,128]{2,1,0:T(8,128)(2,1)}) custom-call(s32[1]{0:T(128)} %bitcast.step_ref.refs_0_, bf16[16,128,256]{2,1,0:T(8,128)(2,1)} %space_block.2.refs_1_, bf16[1728,256]{1,0:T(8,128)(2,1)} %get-tuple-element.16.refs_2_, bf16[768,768]{1,0:T(8,128)(2,1)} %get-tuple-element.17.refs_3_, ...), custom_call_target="tpu_custom_call" | custom-call | tf_op jit(solution)/shard_map/time_block/pallas_call | solution.py:578
  32.6 12.7 %carry.1.latent_ref = f32[256,128]{1,0:T(8,128)} custom-call(bf16[256,128]{1,0:T(8,128)(2,1)} %bitcast.20, f32[256,128]{1,0:T(8,128)} %bitcast.18, f32[256,128]{1,0:T(8,128)} %bitcast.15), custom_call_target="tpu_custom_call" | custom-call | tf_op jit(solution)/shard_map/carry/pallas_call | solution.py:717
  45.3 6.2 %space_block.3.refs_1_ = bf16[16,128,256]{2,1,0:T(8,128)(2,1)} custom-call(f32[16,16,128]{2,1,0:T(8,128)} %bitcast.13, bf16[416,32]{1,0:T(8,128)(2,1)} %get-tuple-element.14.first_ref, f32[408,128]{1,0:T(8,128)} %get-tuple-element.15.offset_ref), custom_call_target="tpu_custom_call" | custom-call | tf_op jit(solution)/shard_map/space_block/pallas_call | solution.py:558
  51.5 15.0 %time_block.3 = (f32[16,16,128]{2,1,0:T(8,128)}, bf16[16,16,128]{2,1,0:T(8,128)(2,1)}) custom-call(s32[1]{0:T(128)} %bitcast.step_ref.refs_0_, bf16[16,128,256]{2,1,0:T(8,128)(2,1)} %space_block.3.refs_1_, bf16[1728,256]{1,0:T(8,128)(2,1)} %get-tuple-element.16.refs_2_, bf16[768,768]{1,0:T(8,128)(2,1)} %get-tuple-element.17.refs_3_, ...), custom_call_target="tpu_custom_call" | custom-call | tf_op jit(solution)/shard_map/time_block/pallas_call | solution.py:578
  66.5 13.4 %carry_last.1 = f32[256,128]{1,0:T(8,128)} custom-call(bf16[256,128]{1,0:T(8,128)(2,1)} %bitcast.19, f32[256,128]{1,0:T(8,128)} %bitcast.17, f32[256,128]{1,0:T(8,128)} %carry.1.latent_ref), custom_call_target="tpu_custom_call" | custom-call | tf_op jit(solution)/shard_map/carry_last/pallas_call | solution.py:717
  79.9 1.6 %copy.14 = f32[16,16,128]{2,1,0:T(8,128)} copy(f32[16,16,128]{2,1,0:T(8,128)} %bitcast.16) | data formatting | bytes 262144

commit v3 on v2

--- a/solution.py
+++ b/solution.py
@@ -15,6 +15,10 @@
 LANES = 128
 INNER = HEADS * HD
 SIDE = math.isqrt(P_SIZE)
+CHUNK = 8
+CARRIED = 2
+SPACE_LAGS = (2, 8, 6)
+TIME_LAGS = (4, 8, 10, 8, 2, 48)
 EPS = 1e-06
 CHANNELS = 16
 WIDE = 2 * LANES
@@ -354,17 +358,33 @@
     interleave(tasks())
 
 
-def time_kernel(lags, fused, *refs):
-    step_ref, token_ref, packed_ref, square_ref, shift_ref, *refs = refs
-    if fused:
-        latent_ref, noise_ref, *rate_refs, increment_ref, sent_ref = refs[:7]
-    else:
-        result_ref = refs[0]
-    predicted_ref = refs[-1]
+def regrid(chunks):
+    count, (_, lanes) = len(chunks), chunks[0].shape
+    block = lane_of(chunks[0].shape) // CHUNK
+    if count * CHUNK != lanes or count & (count - 1):
+        return [
+            beside(*(part[:, index * CHUNK : (index + 1) * CHUNK] for part in chunks))
+            for index in range(lanes // CHUNK)
+        ]
+    chunks, step = list(chunks), 1
+    while step < count:
+        moved = (block & step) != 0
+        for low in range(count):
+            if low & step == 0:
+                first, second = chunks[low], chunks[low + step]
+                chunks[low] = jnp.where(moved, pltpu.roll(second, step * CHUNK, 1), first)
+                chunks[low + step] = jnp.where(
+                    moved, second, pltpu.roll(first, lanes - step * CHUNK, 1)
+                )
+        step *= 2
+    return chunks
+
+
+def time_tasks(lags, token_ref, packed_ref, square_ref, finish, after=lambda group, parts: ()):
     bf16 = jnp.bfloat16
     f32 = jnp.float32
     frames, positions, width = token_ref.shape
-    chunk = 8
+    chunk = CHUNK
     rows = frames * chunk
     size = math.gcd(positions, 2 * chunk)
     parts = size // chunk
@@ -458,8 +478,7 @@
         yield
         predicted = blocks[0][ZERO : ZERO + CHANNELS] * rate
         for part in range(parts):
-            index = (pl.program_id(0) * groups + group) * parts + part
-            predicted_ref[index] = predicted[:, part * rows : (part + 1) * rows]
+            finish(group * parts + part, predicted[:, part * rows : (part + 1) * rows])
 
     def tasks():
         yield group_task(0)
@@ -470,46 +489,123 @@
                     yield group_task(group + 1)
                 yield from (pair_task(group, pair, part) for part in range(parts))
             yield last_task(group)
-
-    interleave(tasks())
-
-    @pl.when(pl.program_id(0) == pl.num_programs(0) - 1)
-    def _():
-        if fused:
-            timestep = step_ref[0]
-            rate_state, rate_denoise, rate_noise = (ref[timestep] for ref in rate_refs)
-            rate_state = rate_state + jnp.where(timestep == 0, 1.0, 0.0)
-        chunks = [predicted_ref[index] for index in range(predicted_ref.shape[0])]
-        block = lane_of(chunks[0].shape) // chunk
-        if len(chunks) == frames and frames & (frames - 1) == 0:
-            step = 1
-            while step < frames:
-                moved = (block & step) != 0
-                for low in range(frames):
-                    if low & step == 0:
-                        first, second = chunks[low], chunks[low + step]
-                        chunks[low] = jnp.where(moved, pltpu.roll(second, step * chunk, 1), first)
-                        chunks[low + step] = jnp.where(
-                            moved, second, pltpu.roll(first, rows - step * chunk, 1)
-                        )
-                step *= 2
-            turned_of = chunks.__getitem__
-        else:
-            def turned_of(frame):
-                return beside(*(part[:, frame * chunk : (frame + 1) * chunk] for part in chunks))
-        for frame in range(frames):
-            turned = turned_of(frame)
-            turned = turned + shift_ref[:, : turned.shape[1]]
-            if fused:
-                turned = (
-                    rate_state * latent_ref[frame]
-                    + rate_denoise * turned
-                    + rate_noise * noise_ref[frame]
-                )
-                increment_ref[frame] = turned
-                sent_ref[frame] = turned.astype(jnp.bfloat16)
-            else:
-                result_ref[frame] = turned
+            yield from after(group, parts)
+
+    return tasks()
+
+
+def time_kernel(lags, token_ref, packed_ref, square_ref, shift_ref, result_ref):
+    chunks = {}
+    interleave(time_tasks(lags, token_ref, packed_ref, square_ref, chunks.__setitem__))
+    for frame, own in enumerate(regrid([chunks[index] for index in sorted(chunks)])):
+        result_ref[frame] = own + shift_ref[:, : own.shape[1]]
+
+
+def step_kernel(
+    lags, last, token_ref, packed_ref, square_ref, shift_ref, latent_ref, noise_ref,
+    state_ref, denoise_ref, scale_ref, out_ref,
+    base_ref, increment_ref, sent_ref, part_ref, total_ref, plane_ref,
+    part_send, part_recv, plane_send, plane_recv,
+):
+    f32 = jnp.float32
+    frames = latent_ref.shape[0]
+    timestep = lax.axis_index("tok")
+    plane, seat = timestep // SIDE, timestep % SIDE
+    hops = range(1, SIDE)
+
+    def in_plane(hop):
+        return {"tok": plane * SIDE + (seat + hop) % SIDE}
+
+    def in_seat(hop):
+        return {"tok": (plane + hop) % SIDE * SIDE + seat}
+
+    barrier = pltpu.get_barrier_semaphore()
+    for hop in hops:
+        for target in (in_plane(hop), in_seat(hop)):
+            pl.semaphore_signal(
+                barrier, inc=1, device_id=target, device_id_type=pl.DeviceIdType.MESH
+            )
+
+    rate_denoise = denoise_ref[timestep]
+    rate_state = state_ref[timestep] + jnp.where(timestep == 0, 1.0, 0.0)
+    rate_noise = scale_ref[timestep]
+    base = [
+        rate_state * latent_ref[frame] + rate_noise * noise_ref[frame] + rate_denoise * shift_ref[...]
+        for frame in range(frames)
+    ]
+    for index, own in enumerate(regrid(base)):
+        base_ref[index] = own
+    pl.semaphore_wait(barrier, 2 * (SIDE - 1))
+
+    done = set()
+
+    def finish(index, predicted):
+        increment = base_ref[index] + rate_denoise * predicted
+        increment_ref[index] = increment
+        sent_ref[index] = increment.astype(jnp.bfloat16)
+        done.add(index)
+
+    def copy(source, target, send, receive, to):
+        return pltpu.make_async_remote_copy(
+            src_ref=source, dst_ref=target, send_sem=send, recv_sem=receive,
+            device_id=to, device_id_type=pl.DeviceIdType.MESH,
+        )
+
+    started = []
+
+    def carry_task(block, own):
+        while not done.issuperset(range(own.start, own.stop)):
+            yield
+        parts = [
+            copy(
+                sent_ref.at[own], part_ref.at[hop - 1, own],
+                part_send.at[hop - 1, block], part_recv.at[hop - 1, block], in_plane(hop),
+            )
+            for hop in hops
+        ]
+        for part in parts:
+            part.start()
+        yield from pause(lags[5])
+        for part in parts:
+            part.wait_recv()
+        total = sent_ref[own].astype(f32)
+        for hop in hops:
+            total = total + part_ref[hop - 1, own].astype(f32)
+        total_ref[own] = total.astype(jnp.bfloat16)
+        planes = [
+            copy(
+                total_ref.at[own], plane_ref.at[hop - 1, own],
+                plane_send.at[hop - 1, block], plane_recv.at[hop - 1, block], in_seat(hop),
+            )
+            for hop in hops
+        ]
+        for part in planes:
+            part.start()
+        started.append((own, parts, planes))
+
+    def after(group, parts):
+        if (group + 1) % CARRIED == 0:
+            block = group // CARRIED
+            yield carry_task(block, slice(block * CARRIED * parts, (block + 1) * CARRIED * parts))
+
+    interleave(time_tasks(lags, token_ref, packed_ref, square_ref, finish, after))
+    chunks = []
+    for own, parts, planes in started:
+        for part in planes:
+            part.wait_recv()
+        for index in range(own.start, own.stop):
+            before = jnp.zeros(latent_ref.shape[1:], f32)
+            for hop in hops:
+                value = plane_ref[hop - 1, index].astype(f32)
+                before = before + jnp.where(plane >= hop, value, 0.0)
+                value = part_ref[hop - 1, index].astype(f32)
+                before = before + jnp.where(seat >= hop, value, 0.0)
+            chunks.append(before + increment_ref[index] if last else before)
+    for frame, own in enumerate(regrid(chunks)):
+        out_ref[frame] = own if last else jnp.where(timestep == 0, latent_ref[frame], own)
+    for own, parts, planes in started:
+        for part in parts + planes:
+            part.wait_send()
 
 
 def whole(array):
@@ -556,7 +652,7 @@
     frames, channels, spatial = latent.shape
     step_frames = math.gcd(frames, 16)
     return pl.pallas_call(
-        functools.partial(space_kernel, (2, 3, 2)),
+        functools.partial(space_kernel, SPACE_LAGS),
         out_shape=jax.ShapeDtypeStruct((frames, spatial, WIDE), jnp.bfloat16),
         grid=(frames // step_frames,),
         in_specs=[
@@ -570,174 +666,47 @@
     )(latent, first, offset)
 
 
-def time_block(own, tokens, packed, square, shift, fused=()):
+def time_block(tokens, packed, square, shift):
     frames, positions, width = tokens.shape
-    step_positions = math.gcd(positions, 64)
-    shape = (frames, CHANNELS, positions)
-    kinds = [jnp.float32] + [jnp.bfloat16] * bool(fused)
     return pl.pallas_call(
-        functools.partial(time_kernel, (2, 2, 3, 2, 1), bool(fused)),
-        out_shape=[jax.ShapeDtypeStruct(shape, kind) for kind in kinds],
-        grid_spec=pltpu.PrefetchScalarGridSpec(
-            num_scalar_prefetch=1,
-            grid=(positions // step_positions,),
-            in_specs=[
-                pl.BlockSpec((frames, step_positions, width), lambda step, own: (0, step, 0)),
-                whole(packed),
-                whole(square),
-                whole(shift),
-            ]
-            + [
-                whole(array) if array.ndim > 1 else pl.BlockSpec(memory_space=pltpu.SMEM)
-                for array in fused
-            ],
-            out_specs=[
-                pl.BlockSpec(shape, lambda step, own: (0, 0, 0), pipeline_mode=pl.Buffered(1))
-                for kind in kinds
-            ],
-            scratch_shapes=[pltpu.VMEM((positions // 8, CHANNELS, frames * 8), jnp.float32)],
-        ),
+        functools.partial(time_kernel, TIME_LAGS),
+        out_shape=jax.ShapeDtypeStruct((frames, CHANNELS, positions), jnp.float32),
+        grid=(1,),
+        in_specs=[whole(array) for array in (tokens, packed, square, shift)],
+        out_specs=whole(jax.ShapeDtypeStruct((frames, CHANNELS, positions), jnp.float32)),
         compiler_params=pltpu.CompilerParams(vmem_limit_bytes=60 * 1024 * 1024),
         name="time_block",
-    )(own, tokens, packed, square, shift, *fused)
-
-
-def carry_kernel(
-    last, groups, sent_ref, increment_ref, latent_ref, out_ref,
-    part_ref, total_ref, plane_ref, early_ref, stage_ref, before_ref,
-    part_send, part_recv, plane_send, plane_recv, stage_send, stage_recv,
-):
-    quarter = part_ref.shape[1]
-    own = lax.axis_index("tok")
-    timestep = own // groups
-    plane, seat = timestep // SIDE, timestep % SIDE
-
-    def device(plane, seat):
-        return {"tok": (plane * SIDE + seat) * groups + own % groups}
-
-    def seat_after(hop):
-        return (seat + hop) % SIDE
-
-    barrier = pltpu.get_barrier_semaphore()
-    for hop in range(1, SIDE):
-        for target in (device(plane, seat_after(hop)), device((plane + hop) % SIDE, seat)):
-            pl.semaphore_signal(
-                barrier, inc=1, device_id=target, device_id_type=pl.DeviceIdType.MESH
-            )
-    pl.semaphore_wait(barrier, 2 * (SIDE - 1))
-
-    def copy(source, target, send, receive, to):
-        return pltpu.make_async_remote_copy(
-            src_ref=source,
-            dst_ref=target,
-            send_sem=send,
-            recv_sem=receive,
-            device_id=to,
-            device_id_type=pl.DeviceIdType.MESH,
-        )
-
-    def rows_of(index):
-        return pl.ds(pl.multiple_of(index * quarter, quarter), quarter)
-
-    parts = []
-    for hop in range(1, SIDE):
-        seat_to = seat_after(hop)
-        parts.append(
-            copy(
-                sent_ref.at[rows_of(seat_to)], part_ref.at[hop - 1],
-                part_send.at[hop - 1], part_recv.at[hop - 1], device(plane, seat_to),
-            )
-        )
-        parts[-1].start()
-    held = [sent_ref[rows_of(seat)].astype(jnp.float32)]
-    for hop in range(1, SIDE):
-        parts[hop - 1].wait_recv()
-        held.append(part_ref[hop - 1].astype(jnp.float32))
-    total_ref[...] = functools.reduce(jnp.add, held).astype(jnp.bfloat16)
-    planes = [
-        copy(
-            total_ref, plane_ref.at[hop - 1], plane_send.at[hop - 1], plane_recv.at[hop - 1],
-            device((plane + hop) % SIDE, seat),
-        )
-        for hop in range(1, SIDE)
-    ]
-    for hop in range(1, SIDE):
-        pl.when(plane + hop < SIDE)(planes[hop - 1].start)
-
-    def earlier_seats(limit):
-        total = jnp.zeros_like(held[0])
-        for hop in range(SIDE):
-            total = total + jnp.where((seat + SIDE - hop) % SIDE < limit, held[hop], 0.0)
-        return total
-
-    early_ref[...] = jnp.zeros_like(early_ref)
-    for hop in range(1, SIDE):
-
-        @pl.when(plane >= hop)
-        def _(hop=hop):
-            planes[hop - 1].wait_recv()
-            early_ref[...] += plane_ref[hop - 1].astype(jnp.float32)
-
-    early = early_ref[...]
-    stages = []
-    for hop in range(1, SIDE):
-        seat_to = seat_after(hop)
-        stage_ref[hop - 1] = early + earlier_seats(seat_to)
-        stages.append(
-            copy(
-                stage_ref.at[hop - 1], before_ref.at[rows_of(seat)],
-                stage_send.at[hop - 1], stage_recv.at[hop - 1], device(plane, seat_to),
-            )
-        )
-        stages[-1].start()
-    own_rows = rows_of(seat)
-
-    def settle(rows, before):
-        if last:
-            out_ref[rows] = before + increment_ref[rows]
-        else:
-            out_ref[rows] = jnp.where(timestep == 0, latent_ref[rows], before)
-
-    settle(own_rows, early + earlier_seats(seat))
-    for hop in range(1, SIDE):
-        stages[hop - 1].wait_recv()
-        rows = rows_of((seat + SIDE - hop) % SIDE)
-        settle(rows, before_ref[rows])
-    for hop in range(1, SIDE):
-        parts[hop - 1].wait_send()
-        pl.when(plane + hop < SIDE)(planes[hop - 1].wait_send)
-        stages[hop - 1].wait_send()
-
-
-def carried_kernel(last, groups, sent, increment, latent):
-    rows, lanes = sent.shape
-    quarter = rows // SIDE
+    )(tokens, packed, square, shift)
+
+
+def step_block(last, tokens, packed, square, shift, latent, noise, rates):
+    frames, positions, width = tokens.shape
     hops = SIDE - 1
+    shape = (positions // CHUNK, CHANNELS, frames * CHUNK)
+    blocks = positions // (2 * CHUNK * CARRIED)
     vmem = pl.BlockSpec(memory_space=pltpu.VMEM)
     return pl.pallas_call(
-        functools.partial(carry_kernel, last, groups),
-        out_shape=jax.ShapeDtypeStruct((rows, lanes), jnp.float32),
-        in_specs=[vmem] * 3,
+        functools.partial(step_kernel, TIME_LAGS, last),
+        out_shape=jax.ShapeDtypeStruct(latent.shape, jnp.float32),
+        in_specs=[vmem] * 6 + [pl.BlockSpec(memory_space=pltpu.SMEM)] * 3,
         out_specs=vmem,
         scratch_shapes=[
-            pltpu.VMEM((hops, quarter, lanes), jnp.bfloat16),
-            pltpu.VMEM((quarter, lanes), jnp.bfloat16),
-            pltpu.VMEM((hops, quarter, lanes), jnp.bfloat16),
-            pltpu.VMEM((quarter, lanes), jnp.float32),
-            pltpu.VMEM((hops, quarter, lanes), jnp.float32),
-            pltpu.VMEM((rows, lanes), jnp.float32),
+            pltpu.VMEM(shape, jnp.float32),
+            pltpu.VMEM(shape, jnp.float32),
+            pltpu.VMEM(shape, jnp.bfloat16),
+            pltpu.VMEM((hops,) + shape, jnp.bfloat16),
+            pltpu.VMEM(shape, jnp.bfloat16),
+            pltpu.VMEM((hops,) + shape, jnp.bfloat16),
         ]
-        + [pltpu.SemaphoreType.DMA((hops,))] * 6,
-        compiler_params=pltpu.CompilerParams(collective_id=int(last), has_side_effects=True),
-        name="carry_last" if last else "carry",
-    )(sent, increment, latent)
+        + [pltpu.SemaphoreType.DMA((hops, blocks))] * 4,
+        compiler_params=pltpu.CompilerParams(
+            collective_id=int(last), has_side_effects=True, vmem_limit_bytes=60 * 1024 * 1024
+        ),
+        name="step_last" if last else "step",
+    )(tokens, packed, square, shift, latent, noise, *rates)
 
 
 def carried_in(last, groups, same_block, timestep, sent, increment, latent):
-    rows = sent.size // LANES
-    if sent.shape[-1] == LANES and rows % (SIDE * 16) == 0:
-        flat = [array.reshape(rows, LANES) for array in (sent, increment, latent)]
-        return carried_kernel(last, groups, *flat).reshape(latent.shape)
     gathered = lax.all_gather(
         sent, "tok", axis_index_groups=same_block if groups > 1 else None
     )
@@ -775,15 +744,14 @@
     latent = initial_guess
     for iteration in range(ITERS):
         tokens = space_block(latent, first, offset)
+        last = iteration == ITERS - 1
         if groups == 1:
-            increment, sent = time_block(
-                own, tokens, packed, square, shift, (latent, noise_draws) + rates
-            )
+            latent = step_block(last, tokens, packed, square, shift, latent, noise_draws, rates)
         else:
             tokens = lax.all_to_all(
                 tokens, "tok", split_axis=1, concat_axis=0, axis_index_groups=same_step, tiled=True
             )
-            (predicted,) = time_block(own, tokens, packed, square, shift)
+            predicted = time_block(tokens, packed, square, shift)
             predicted = lax.all_to_all(
                 predicted, "tok", split_axis=0, concat_axis=2, axis_index_groups=same_step, tiled=True
             )
@@ -793,9 +761,7 @@
             rate_state = rate_state + jnp.where(timestep == 0, 1.0, 0.0)
             increment = rate_state * latent + rate_denoise * predicted + rate_noise * noise_draws
             sent = increment.astype(jnp.bfloat16)
-        latent = carried_in(
-            iteration == ITERS - 1, groups, same_block, timestep, sent, increment, latent
-        )
+            latent = carried_in(last, groups, same_block, timestep, sent, increment, latent)
     return latent
 
 

time: 82.7 us -> 65.3 us (0.79); the launches traced: 81.4 us -> 65.1 us
  Pallas kernels: 79.9 us -> 63.5 us
    pallas_call x6 -> x4, Pallas kernels: 68.4 us -> 52 us  [the longest x2 41.6 us: step_block(): pl.pallas_call(functools.partial(step_kernel, TIME_LAGS, last), out_shape...]
where the time goes in v3:
time: 65.3 us; the launch traced here: 65.1 us
  Pallas kernels  63.5 us (97%)
  local copies, waits for them, and re-layouts  1.57 us (2%)
    pallas_call x2, Pallas kernels, step_block(): pl.pallas_call(functools.partial(step_kernel, TIME_LAGS, last), out_shape...  41.6 us
    pallas_call x1, Pallas kernels, fold(): pl.pallas_call(fold_kernel, out_shape=[jax.ShapeDtypeStruct(*shape) for s...  11.4 us
    pallas_call x2, Pallas kernels, space_block(): pl.pallas_call(functools.partial(space_kernel, SPACE_LAGS), out_shape=jax...  10.5 us
    unnamed x1, local copies, waits for them, and re-layouts  1.57 us

profile of v3, /device:TPU:0, one launch (start us, length us, event | category | flops | bytes accessed | tf_op | source)
XLA Modules:
  0.0 65.1 jit_solution(10943110918511262221)
XLA Ops:
  0.0 11.4 %fold.1 = (bf16[416,32]{1,0:T(8,128)(2,1)}, f32[408,128]{1,0:T(8,128)}, bf16[1728,256]{1,0:T(8,128)(2,1)}, bf16[768,768]{1,0:T(8,128)(2,1)}, f32[16,128]{1,0:T(8,128)}) custom-call(s32[1]{0:T(128)} %bitcast.step_ref, f32[16,8,1152]{2,1,0:T(8,128)} %table_ref.1, bf16[16,1152]{1,0:T(8,128)(2,1)} %embed_ref.1, bf16[1728,1152]{1,0:T(8,128)(2,1)} %bitcast.4, ...), custom_call_target="tpu_custom_call" | custom-call | tf_op jit(solution)/shard_map/fold/pallas_call | solution.py:626
  11.4 5.2 %space_block.2.token_ref = bf16[16,128,256]{2,1,0:T(8,128)(2,1)} custom-call(f32[16,16,128]{2,1,0:T(8,128)} %latent_ref.3, bf16[416,32]{1,0:T(8,128)(2,1)} %get-tuple-element.10.first_ref, f32[408,128]{1,0:T(8,128)} %get-tuple-element.11.offset_ref), custom_call_target="tpu_custom_call" | custom-call | tf_op jit(solution)/shard_map/space_block/pallas_call | solution.py:654
  16.7 22.0 %step.1.latent_ref = f32[16,16,128]{2,1,0:T(8,128)} custom-call(bf16[16,128,256]{2,1,0:T(8,128)(2,1)} %space_block.2.token_ref, bf16[1728,256]{1,0:T(8,128)(2,1)} %get-tuple-element.12.packed_ref, bf16[768,768]{1,0:T(8,128)(2,1)} %get-tuple-element.13.square_ref, f32[16,128]{1,0:T(8,128)} %get-tuple-element.14.shift_ref, f32[16,16,128]{2,1,0:T(8,128)} %latent_ref.3, ...), custom_call_target="tpu_custom_call" | custom-call | tf_op jit(solution)/shard_map/step/pallas_call | solution.py:688
  38.7 5.2 %space_block.3.token_ref = bf16[16,128,256]{2,1,0:T(8,128)(2,1)} custom-call(f32[16,16,128]{2,1,0:T(8,128)} %step.1.latent_ref, bf16[416,32]{1,0:T(8,128)(2,1)} %get-tuple-element.10.first_ref, f32[408,128]{1,0:T(8,128)} %get-tuple-element.11.offset_ref), custom_call_target="tpu_custom_call" | custom-call | tf_op jit(solution)/shard_map/space_block/pallas_call | solution.py:654
  43.9 19.5 %step_last.1 = f32[16,16,128]{2,1,0:T(8,128)} custom-call(bf16[16,128,256]{2,1,0:T(8,128)(2,1)} %space_block.3.token_ref, bf16[1728,256]{1,0:T(8,128)(2,1)} %get-tuple-element.12.packed_ref, bf16[768,768]{1,0:T(8,128)(2,1)} %get-tuple-element.13.square_ref, f32[16,128]{1,0:T(8,128)} %get-tuple-element.14.shift_ref, f32[16,16,128]{2,1,0:T(8,128)} %step.1.latent_ref, ...), custom_call_target="tpu_custom_call" | custom-call | tf_op jit(solution)/shard_map/step_last/pallas_call | solution.py:688
  63.5 1.6 %copy.14 = f32[16,16,128]{2,1,0:T(8,128)} copy(f32[16,16,128]{2,1,0:T(8,128)} %step_last.1) | data formatting | bytes 262144

commit v4 on v3

--- a/solution.py
+++ b/solution.py
@@ -18,6 +18,8 @@
 CHUNK = 8
 CARRIED = 2
 SPACE_LAGS = (2, 8, 6)
+FOLD_LAG = 4
+FOLD_EVERY = 3
 TIME_LAGS = (4, 8, 10, 8, 2, 48)
 EPS = 1e-06
 CHANNELS = 16
@@ -73,56 +75,72 @@
     return jnp.where(lane_of(spread.shape) // HD == head, spread, 0.0)
 
 
-def fold_kernel(
-    step_ref, table_ref, embed_ref, space_in_ref, space_out_ref, time_in_ref, time_out_ref, final_ref,
-    first_ref, offset_ref, packed_ref, square_ref, shift_ref, lines_ref,
-):
-    def table(row):
-        return table_ref[row : row + 1, :]
-
-    def zeros(rows, width=None):
-        return jnp.zeros((rows, width or table_ref.shape[1]), jnp.float32)
-
-    highest = lax.Precision.HIGHEST
-    features = table_ref.shape[1]
+def stack(*parts):
+    return jnp.concatenate(parts, axis=0)
+
+
+def beside(*parts):
+    return jnp.concatenate(parts, axis=1)
+
+
+def on_diagonal(first, second):
+    blank = jnp.zeros_like(first)
+    return stack(beside(first, blank), beside(blank, second))
+
+
+def interleave(tasks):
+    tasks, running = list(tasks), []
+    while tasks or running:
+        running += [tasks.pop(0)] if tasks else []
+        running = [task for task in running if next(task, tasks) is not tasks]
+
+
+def pause(turns):
+    for turn in range(turns):
+        yield
+
+
+def wait_for(state, key):
+    while key not in state:
+        yield
+
+
+def fold_first(arrive, table, embed_ref, space_in_ref, first_ref, offset_ref):
     embed = centred(embed_ref[...].astype(jnp.float32))
-    lines = embed * (1.0 + table(1))
-    shift = jnp.concatenate([table(0), zeros(7)], axis=0)
-    high, low = halves(lines)
-    shift_high, shift_low = halves(shift)
-    tail = jnp.concatenate([shift_high.astype(jnp.float32), shift_low.astype(jnp.float32)], axis=0)
-    folded = dot_rows(
-        jnp.concatenate([high, low, tail.astype(jnp.bfloat16)], axis=0), space_in_ref[...]
-    )
+    features = embed.shape[1]
+
+    def zeros(rows, width=features):
+        return jnp.zeros((rows, width), jnp.float32)
+
+    arrive("table")
+    lines = stack(*halves(embed * (1.0 + table(1))))
+    tail = stack(*(half.astype(jnp.float32) for half in halves(stack(table(0), zeros(7)))))
+    arrive("space_in")
+    folded = dot_rows(stack(lines, tail.astype(jnp.bfloat16)), space_in_ref[...])
     lat = folded[:CHANNELS] + folded[CHANNELS : 2 * CHANNELS]
     const = folded[2 * CHANNELS : 2 * CHANNELS + 8] + folded[2 * CHANNELS + 8 :]
 
     def part(values, which):
         return values[:, which * INNER : (which + 1) * INNER]
 
+    def fine(rows, side):
+        high, low = halves(rows)
+        side_high, side_low = halves(side)
+        both = dot_rows(high, stack(side_high, side_low))
+        return both[:, :LANES] + both[:, LANES:] + dot_rows(low, side_high)
+
+    def side_of(rows, point):
+        width = rows.shape[1]
+        return stack(rows, rows, point, zeros(7, width), zeros(LANES - 2 * CHANNELS - 8, width))
+
     query, key, value = (part(lat, which) for which in range(3))
     query_c, key_c, value_c = (part(const, which)[:1] for which in range(3))
-    key_side = jnp.concatenate([key, key, key_c, zeros(7, INNER)], axis=0)
-    query_side = jnp.concatenate([query, query, query_c, zeros(7, INNER)], axis=0)
-    scores = dot_rows(
-        jnp.concatenate([by_head(query, "hc"), by_head(query_c, "ch")], axis=0) * SCALE,
-        key_side, highest,
-    )
-    key_square = dot_rows(
-        jnp.concatenate([by_head(key, "ch"), by_head(key_c, "ch")], axis=0) * (1.0 / HD),
-        key_side, highest,
-    )
-    query_square = dot_rows(
-        jnp.concatenate([by_head(query, "ch"), by_head(query_c, "ch")], axis=0) * (1.0 / HD),
-        query_side, highest,
-    )
-    gram = dot_rows(embed, jnp.concatenate([embed, embed, zeros(8)], axis=0), highest) * (
-        1.0 / features
-    )
-    first = jnp.concatenate(
-        [scores, key_square[:ROWS_T], query_square[:ROWS_T], gram, zeros(8, 2 * CHANNELS + 8)],
-        axis=0,
-    )
+    key_side, query_side = side_of(key, key_c), side_of(query, query_c)
+    scores = fine(stack(by_head(query, "hc"), by_head(query_c, "ch")) * SCALE, key_side)
+    key_square = fine(stack(by_head(key, "ch"), by_head(key_c, "ch")) * (1.0 / HD), key_side)
+    query_square = fine(stack(by_head(query, "ch"), by_head(query_c, "ch")) * (1.0 / HD), query_side)
+    gram = fine(embed, side_of(embed, zeros(1))) * (1.0 / features)
+    first = stack(scores, key_square[:ROWS_T], query_square[:ROWS_T], gram, zeros(8, LANES))
     high, low = halves(first)
     upper = lane_of(first.shape) < CHANNELS
     chosen = jnp.where(upper, high.astype(jnp.float32), low.astype(jnp.float32))
@@ -137,124 +155,139 @@
         offset_ref[start + ROWS_T : start + ROWS_T + 8] = jnp.broadcast_to(
             square[ROWS_T:, point : point + 1], (8, LANES)
         )
-
-    value_high, value_low = halves(by_head(value, "hc"))
-    const_high, const_low = halves(jnp.concatenate([value_c, zeros(7, INNER)], axis=0))
-    tail = jnp.concatenate([const_high.astype(jnp.float32), const_low.astype(jnp.float32)], axis=0)
-    mixed = dot(
-        jnp.concatenate([value_high, value_low, tail.astype(jnp.bfloat16)], axis=0),
-        space_out_ref[...],
-    )
-    gate = table(2)
-    attended = centred(gate * (mixed[:ROWS_T] + mixed[ROWS_T : 2 * ROWS_T]))
-    point = centred(gate * (mixed[2 * ROWS_T : 2 * ROWS_T + 8] + mixed[2 * ROWS_T + 8 :]))
-
-    scaled = 1.0 + table(4)
-    lat_high, lat_low = halves(embed * scaled)
-    ends = jnp.concatenate([table(3), point[:1] * scaled, zeros(6)], axis=0)
-    ends_high, ends_low = halves(ends)
-    tail = jnp.concatenate([ends_high.astype(jnp.float32), ends_low.astype(jnp.float32)], axis=0)
-    rows = jnp.concatenate(
-        [(attended * scaled).astype(jnp.bfloat16), lat_high, lat_low, tail.astype(jnp.bfloat16)],
-        axis=0,
-    )
+    values = stack(*halves(by_head(value, "hc")))
+    tail = stack(*(half.astype(jnp.float32) for half in halves(stack(value_c, zeros(7, INNER)))))
+    return embed, stack(values, tail.astype(jnp.bfloat16))
+
+
+def fold_tasks(
+    lag, arrive, table, embed, values, space_out_ref, time_in_ref, time_out_ref, final_ref,
+    packed_ref, square_ref, shift_ref, lines_ref,
+):
+    f32 = jnp.float32
+    bf16 = jnp.bfloat16
+    features = embed.shape[1]
+    state = {"mixed": {}, "lines": set()}
+
+    def zeros(rows, width=features):
+        return jnp.zeros((rows, width), f32)
+
+    def mixed_task(start):
+        if start == 0:
+            arrive("space_out")
+        own = dot(values, space_out_ref[:, start : min(start + WIDE, features)])
+        yield from pause(lag)
+        state["mixed"][start] = own
+
+    def rows_task():
+        starts = range(0, features, WIDE)
+        while len(state["mixed"]) < len(starts):
+            yield
+        mixed = beside(*(state["mixed"][start] for start in starts))
+        gate = table(2)
+        attended = centred(gate * (mixed[:ROWS_T] + mixed[ROWS_T : 2 * ROWS_T]))
+        point = centred(gate * (mixed[2 * ROWS_T : 2 * ROWS_T + 8] + mixed[2 * ROWS_T + 8 :]))
+        yield
+        scaled = 1.0 + table(4)
+        ends = halves(stack(table(3), point[:1] * scaled, zeros(6)))
+        tail = stack(*(half.astype(f32) for half in ends))
+        state["rows"] = stack(
+            (attended * scaled).astype(bf16), *halves(embed * scaled), tail.astype(bf16)
+        )
+        lines_ref[:LAT] = attended.astype(bf16)
+        high, low = halves(embed)
+        lines_ref[LAT:DUP] = high
+        lines_ref[DUP:ZERO] = low
+        point = (half.astype(f32) for half in halves(point[:1]))
+        lines_ref[ZERO:ATT] = stack(zeros(ONE - ZERO), *point, zeros(ATT - ONE - 2)).astype(bf16)
+        state["lines"].add("tokens")
 
     def settle(columns):
         lat = columns[LAT:DUP] + columns[DUP : DUP + CHANNELS]
-        lat_high = lat.astype(jnp.bfloat16).astype(jnp.float32)
+        lat_high = lat.astype(bf16).astype(f32)
         ends = columns[DUP + CHANNELS : DUP + CHANNELS + 8] + columns[DUP + CHANNELS + 8 :]
-        ends_high = ends.astype(jnp.bfloat16).astype(jnp.float32)
+        ends_high = ends.astype(bf16).astype(f32)
         ends_low = ends - ends_high
         width = columns.shape[1]
-        return jnp.concatenate(
-            [
-                columns[:LAT], lat_high, lat - lat_high,
-                ends_high[:1], ends_high[:1], ends_low[:1], zeros(ONE - ZERO - 3, width),
-                ends_high[1:2], ends_low[1:2], zeros(WIDE - ONE - 2, width),
-            ],
-            axis=0,
-        ).astype(jnp.bfloat16)
-
-    for which in range(3):
-        own = slice(which * INNER, (which + 1) * INNER)
-        packed_ref[own] = settle(dot_rows(rows, time_in_ref[own, :])).T
-
-    gate = table(5)
-    lat_high, lat_low = halves(embed)
-    point_high, point_low = halves(point[:1])
-    lines_ref[:LAT] = attended.astype(jnp.bfloat16)
-    lines_ref[LAT:DUP] = lat_high
-    lines_ref[DUP:ZERO] = lat_low
-    lines_ref[ZERO:ATT] = jnp.concatenate(
-        [
-            zeros(ONE - ZERO), point_high.astype(jnp.float32), point_low.astype(jnp.float32),
-            zeros(ATT - ONE - 2),
-        ],
-        axis=0,
-    ).astype(jnp.bfloat16)
-    lines_ref[ATT:WIDE] = centred(gate * time_out_ref[BASE:].astype(jnp.float32)).astype(jnp.bfloat16)
-    for start in range(0, BASE, LANES):
-        lines_ref[WIDE + start : WIDE + start + LANES] = centred(
-            gate * time_out_ref[start : start + LANES].astype(jnp.float32)
-        ).astype(jnp.bfloat16)
-    final = final_ref[...].astype(jnp.float32)
-    shift_ref[...] = jnp.broadcast_to(
-        jnp.sum(final * table(6), -1, keepdims=True), (CHANNELS, LANES)
+        return stack(
+            columns[:LAT], lat_high, lat - lat_high,
+            ends_high[:1], ends_high[:1], ends_low[:1], zeros(ONE - ZERO - 3, width),
+            ends_high[1:2], ends_low[1:2], zeros(WIDE - ONE - 2, width),
+        ).astype(bf16)
+
+    def packed_task(start):
+        yield from wait_for(state, "rows")
+        if start == 0:
+            arrive("time_in")
+        own = slice(start, min(start + WIDE, 3 * INNER))
+        columns = dot_rows(state["rows"], time_in_ref[own, :])
+        yield from pause(lag)
+        packed_ref[own] = settle(columns).T
+
+    def lines_task(start):
+        arrive("time_out")
+        gate = table(5)
+        if start == BASE:
+            own, target = slice(BASE, INNER), ATT
+        else:
+            own, target = slice(start, start + LANES), WIDE + start
+        rows = centred(gate * time_out_ref[own].astype(f32))
+        lines_ref[target : target + rows.shape[0]] = rows.astype(bf16)
+        state["lines"].add(start)
+        yield
+
+    tiles = lines_ref.shape[0] // WIDE
+
+    def square_task(column, row):
+        while len(state["lines"]) < 2 + BASE // LANES:
+            yield
+        other = lines_ref[column * WIDE : (column + 1) * WIDE]
+        if column == 0:
+            final = final_ref[...].astype(f32)
+            if row == 0:
+                shift_ref[...] = jnp.broadcast_to(
+                    jnp.sum(final * table(6), -1, keepdims=True), (CHANNELS, LANES)
+                )
+            final = (final * (1.0 + table(7))).astype(bf16)
+            other = stack(other[:ZERO], final, other[ZERO + CHANNELS :])
+        block = dot_rows(other, lines_ref[row * WIDE : (row + 1) * WIDE])
+        yield from pause(lag)
+        gain = (1.0 if row == column else 2.0) / features
+        if column == 0:
+            line = row_of((WIDE, 1))
+            gain = jnp.where((line >= ZERO) & (line < ZERO + CHANNELS), 1.0, gain)
+        square_ref[column * WIDE : (column + 1) * WIDE, row * WIDE : (row + 1) * WIDE] = (
+            (block * gain).astype(bf16)
+        )
+
+    starts = range(0, features, WIDE)
+    yield from (mixed_task(start) for start in starts)
+    yield rows_task()
+    yield from (lines_task(start) for start in range(0, BASE + 1, LANES))
+    yield from (packed_task(start) for start in range(0, 3 * INNER, WIDE))
+    yield from (square_task(column, row) for column in range(tiles) for row in range(column, tiles))
+
+
+def fold_kernel(
+    step_ref, table_ref, embed_ref, space_in_ref, space_out_ref, time_in_ref, time_out_ref, final_ref,
+    first_ref, offset_ref, packed_ref, square_ref, shift_ref, lines_ref,
+):
+    def table(row):
+        return table_ref[row : row + 1, :]
+
+    def arrive(name):
+        pass
+
+    embed, values = fold_first(arrive, table, embed_ref, space_in_ref, first_ref, offset_ref)
+    interleave(
+        fold_tasks(
+            3, arrive, table, embed, values, space_out_ref, time_in_ref, time_out_ref, final_ref,
+            packed_ref, square_ref, shift_ref, lines_ref,
+        )
     )
-    base = jnp.concatenate(
-        [
-            lines_ref[:ZERO],
-            (final * (1.0 + table(7))).astype(jnp.bfloat16),
-            lines_ref[ZERO + CHANNELS : WIDE],
-        ],
-        axis=0,
-    )
-    line = row_of((WIDE, 1))
-    plain = (line >= ZERO) & (line < ZERO + CHANNELS)
-    tiles = lines_ref.shape[0] // WIDE
-    for column in range(tiles):
-        other = lines_ref[column * WIDE : (column + 1) * WIDE] if column else base
-        for row in range(column, tiles):
-            block = dot_rows(other, lines_ref[row * WIDE : (row + 1) * WIDE])
-            block = block * ((1.0 if row == column else 2.0) / features) if column else (
-                block * jnp.where(plain, 1.0, (1.0 if row == column else 2.0) / features)
-            )
-            square_ref[column * WIDE : (column + 1) * WIDE, row * WIDE : (row + 1) * WIDE] = (
-                block.astype(jnp.bfloat16)
-            )
-
-
-def stack(*parts):
-    return jnp.concatenate(parts, axis=0)
-
-
-def beside(*parts):
-    return jnp.concatenate(parts, axis=1)
-
-
-def on_diagonal(first, second):
-    blank = jnp.zeros_like(first)
-    return stack(beside(first, blank), beside(blank, second))
-
-
-def interleave(tasks):
-    tasks, running = list(tasks), []
-    while tasks or running:
-        running += [tasks.pop(0)] if tasks else []
-        running = [task for task in running if next(task, tasks) is not tasks]
-
-
-def pause(turns):
-    for turn in range(turns):
-        yield
-
-
-def wait_for(state, key):
-    while key not in state:
-        yield
-
-
-def space_kernel(lags, latent_ref, first_ref, offset_ref, token_ref):
+
+
+def space_tasks(lags, latent_ref, first_ref, offset_ref, token_ref):
     frames, channels, spatial = latent_ref.shape
     bf16 = jnp.bfloat16
     f32 = jnp.float32
@@ -355,7 +388,11 @@
             if frame >= 0:
                 yield from (pair_task(frame, pair) for pair in range(HEADS // 2))
 
-    interleave(tasks())
+    return tasks()
+
+
+def space_kernel(lags, *refs):
+    interleave(space_tasks(lags, *refs))
 
 
 def regrid(chunks):
@@ -501,17 +538,44 @@
         result_ref[frame] = own + shift_ref[:, : own.shape[1]]
 
 
-def step_kernel(
-    lags, last, token_ref, packed_ref, square_ref, shift_ref, latent_ref, noise_ref,
-    state_ref, denoise_ref, scale_ref, out_ref,
-    base_ref, increment_ref, sent_ref, part_ref, total_ref, plane_ref,
-    part_send, part_recv, plane_send, plane_recv,
+def merged(tasks, others, every):
+    others = list(others)
+    for index, task in enumerate(tasks):
+        yield task
+        if others and index % every == every - 1:
+            yield others.pop(0)
+    yield from others
+
+
+def sampler_kernel(
+    table_from, embed_ref, space_in_from, space_out_from, time_in_from, time_out_from, final_ref,
+    latent_ref, noise_ref, state_ref, denoise_ref, scale_ref, out_ref,
+    table_ref, space_in_ref, space_out_ref, time_in_ref, time_out_ref,
+    first_ref, offset_ref, packed_ref, square_ref, shift_ref, lines_ref, token_ref,
+    own_ref, fresh_ref, running_ref, increment_ref, sent_ref, part_ref, total_ref, plane_ref,
+    load_sem, part_send, part_recv, plane_send, plane_recv,
 ):
     f32 = jnp.float32
+    bf16 = jnp.bfloat16
     frames = latent_ref.shape[0]
     timestep = lax.axis_index("tok")
     plane, seat = timestep // SIDE, timestep % SIDE
     hops = range(1, SIDE)
+
+    loads = {
+        name: pltpu.make_async_copy(source, target, load_sem.at[index])
+        for index, (name, source, target) in enumerate(
+            (
+                ("table", table_from.at[timestep], table_ref),
+                ("space_in", space_in_from, space_in_ref),
+                ("space_out", space_out_from, space_out_ref),
+                ("time_out", time_out_from, time_out_ref),
+                ("time_in", time_in_from, time_in_ref),
+            )
+        )
+    }
+    for load in loads.values():
+        load.start()
 
     def in_plane(hop):
         return {"tok": plane * SIDE + (seat + hop) % SIDE}
@@ -526,24 +590,20 @@
                 barrier, inc=1, device_id=target, device_id_type=pl.DeviceIdType.MESH
             )
 
+    def arrive(name):
+        if name in loads:
+            loads.pop(name).wait()
+
+    def table(row):
+        return table_ref[row : row + 1, :]
+
     rate_denoise = denoise_ref[timestep]
     rate_state = state_ref[timestep] + jnp.where(timestep == 0, 1.0, 0.0)
     rate_noise = scale_ref[timestep]
-    base = [
-        rate_state * latent_ref[frame] + rate_noise * noise_ref[frame] + rate_denoise * shift_ref[...]
-        for frame in range(frames)
-    ]
-    for index, own in enumerate(regrid(base)):
-        base_ref[index] = own
-    pl.semaphore_wait(barrier, 2 * (SIDE - 1))
-
-    done = set()
-
-    def finish(index, predicted):
-        increment = base_ref[index] + rate_denoise * predicted
-        increment_ref[index] = increment
-        sent_ref[index] = increment.astype(jnp.bfloat16)
-        done.add(index)
+    for target, source in ((running_ref, latent_ref), (fresh_ref, noise_ref)):
+        for index, own in enumerate(regrid([source[frame] for frame in range(frames)])):
+            target[index] = own
+    embed, values = fold_first(arrive, table, embed_ref, space_in_ref, first_ref, offset_ref)
 
     def copy(source, target, send, receive, to):
         return pltpu.make_async_remote_copy(
@@ -551,61 +611,89 @@
             device_id=to, device_id_type=pl.DeviceIdType.MESH,
         )
 
-    started = []
-
-    def carry_task(block, own):
-        while not done.issuperset(range(own.start, own.stop)):
-            yield
-        parts = [
-            copy(
-                sent_ref.at[own], part_ref.at[hop - 1, own],
-                part_send.at[hop - 1, block], part_recv.at[hop - 1, block], in_plane(hop),
+    sent = []
+    for iteration in range(ITERS):
+        last = iteration == ITERS - 1
+        source_ref = own_ref if iteration else latent_ref
+        spread = space_tasks(SPACE_LAGS, source_ref, first_ref, offset_ref, token_ref)
+        if iteration == 0:
+            others = fold_tasks(
+                FOLD_LAG, arrive, table, embed, values, space_out_ref, time_in_ref, time_out_ref,
+                final_ref, packed_ref, square_ref, shift_ref, lines_ref,
             )
-            for hop in hops
-        ]
-        for part in parts:
-            part.start()
-        yield from pause(lags[5])
-        for part in parts:
-            part.wait_recv()
-        total = sent_ref[own].astype(f32)
-        for hop in hops:
-            total = total + part_ref[hop - 1, own].astype(f32)
-        total_ref[own] = total.astype(jnp.bfloat16)
-        planes = [
-            copy(
-                total_ref.at[own], plane_ref.at[hop - 1, own],
-                plane_send.at[hop - 1, block], plane_recv.at[hop - 1, block], in_seat(hop),
-            )
-            for hop in hops
-        ]
-        for part in planes:
-            part.start()
-        started.append((own, parts, planes))
-
-    def after(group, parts):
-        if (group + 1) % CARRIED == 0:
-            block = group // CARRIED
-            yield carry_task(block, slice(block * CARRIED * parts, (block + 1) * CARRIED * parts))
-
-    interleave(time_tasks(lags, token_ref, packed_ref, square_ref, finish, after))
-    chunks = []
-    for own, parts, planes in started:
-        for part in planes:
-            part.wait_recv()
-        for index in range(own.start, own.stop):
-            before = jnp.zeros(latent_ref.shape[1:], f32)
+            spread = merged(spread, others, FOLD_EVERY)
+        interleave(spread)
+        if iteration == 0:
+            pl.semaphore_wait(barrier, 2 * (SIDE - 1))
+        done, started = set(), []
+
+        def finish(index, predicted):
+            increment = rate_denoise * (predicted + shift_ref[...])
+            increment = increment + rate_noise * fresh_ref[index] + rate_state * running_ref[index]
+            increment_ref[index] = increment
+            sent_ref[iteration, index] = increment.astype(bf16)
+            done.add(index)
+
+        def carry_task(block, own):
+            while not done.issuperset(range(own.start, own.stop)):
+                yield
+            parts = [
+                copy(
+                    sent_ref.at[iteration, own], part_ref.at[iteration, hop - 1, own],
+                    part_send.at[iteration, hop - 1, block], part_recv.at[iteration, hop - 1, block],
+                    in_plane(hop),
+                )
+                for hop in hops
+            ]
+            for part in parts:
+                part.start()
+            yield from pause(TIME_LAGS[5])
+            for part in parts:
+                part.wait_recv()
+            total = sent_ref[iteration, own].astype(f32)
             for hop in hops:
-                value = plane_ref[hop - 1, index].astype(f32)
-                before = before + jnp.where(plane >= hop, value, 0.0)
-                value = part_ref[hop - 1, index].astype(f32)
-                before = before + jnp.where(seat >= hop, value, 0.0)
-            chunks.append(before + increment_ref[index] if last else before)
-    for frame, own in enumerate(regrid(chunks)):
-        out_ref[frame] = own if last else jnp.where(timestep == 0, latent_ref[frame], own)
-    for own, parts, planes in started:
-        for part in parts + planes:
-            part.wait_send()
+                total = total + part_ref[iteration, hop - 1, own].astype(f32)
+            total_ref[iteration, own] = total.astype(bf16)
+            planes = [
+                copy(
+                    total_ref.at[iteration, own], plane_ref.at[iteration, hop - 1, own],
+                    plane_send.at[iteration, hop - 1, block], plane_recv.at[iteration, hop - 1, block],
+                    in_seat(hop),
+                )
+                for hop in hops
+            ]
+            for part in planes:
+                part.start()
+            started.append((own, planes))
+            sent.extend(parts + planes)
+
+        def after(group, parts):
+            if (group + 1) % CARRIED == 0:
+                block = group // CARRIED
+                yield carry_task(block, slice(block * CARRIED * parts, (block + 1) * CARRIED * parts))
+
+        interleave(time_tasks(TIME_LAGS, token_ref, packed_ref, square_ref, finish, after))
+        chunks = []
+        for own, planes in started:
+            for part in planes:
+                part.wait_recv()
+            for index in range(own.start, own.stop):
+                before = jnp.zeros(latent_ref.shape[1:], f32)
+                for hop in hops:
+                    value = plane_ref[iteration, hop - 1, index].astype(f32)
+                    before = before + jnp.where(plane >= hop, value, 0.0)
+                    value = part_ref[iteration, hop - 1, index].astype(f32)
+                    before = before + jnp.where(seat >= hop, value, 0.0)
+                if last:
+                    chunks.append(before + increment_ref[index])
+                else:
+                    chunks.append(jnp.where(timestep == 0, running_ref[index], before))
+                    running_ref[index] = chunks[-1]
+        target_ref = out_ref if last else own_ref
+        for frame, own in enumerate(regrid(chunks)):
+            target_ref[frame] = own
+    for part in sent:
+        part.wait_send()
 
 
 def whole(array):
@@ -679,31 +767,48 @@
     )(tokens, packed, square, shift)
 
 
-def step_block(last, tokens, packed, square, shift, latent, noise, rates):
-    frames, positions, width = tokens.shape
+def sampler(modulation, weights, latent, noise, rates):
+    embed, space_in, space_out, time_in, time_out, final = weights
+    frames, channels, positions = latent.shape
+    features = embed.shape[1]
     hops = SIDE - 1
-    shape = (positions // CHUNK, CHANNELS, frames * CHUNK)
+    shape = (positions // CHUNK, channels, frames * CHUNK)
     blocks = positions // (2 * CHUNK * CARRIED)
-    vmem = pl.BlockSpec(memory_space=pltpu.VMEM)
+    vmem, anywhere = (pl.BlockSpec(memory_space=space) for space in (pltpu.VMEM, pl.ANY))
+    f32, bf16 = jnp.float32, jnp.bfloat16
+    scratch = [(modulation.shape[1:], f32)]
+    scratch += [(weight.shape, bf16) for weight in (space_in, space_out, time_in, time_out)]
+    scratch += [
+        ((ROWS_AA, 2 * CHANNELS), bf16),
+        ((3 * (ROWS_T + 8), LANES), f32),
+        ((3 * INNER, WIDE), bf16),
+        ((BASE + WIDE, BASE + WIDE), bf16),
+        ((CHANNELS, LANES), f32),
+        ((BASE + WIDE, features), bf16),
+        ((frames, positions, WIDE), bf16),
+        (latent.shape, f32),
+        (shape, f32),
+        (shape, f32),
+        (shape, f32),
+        ((ITERS,) + shape, bf16),
+        ((ITERS, hops) + shape, bf16),
+        ((ITERS,) + shape, bf16),
+        ((ITERS, hops) + shape, bf16),
+    ]
     return pl.pallas_call(
-        functools.partial(step_kernel, TIME_LAGS, last),
-        out_shape=jax.ShapeDtypeStruct(latent.shape, jnp.float32),
-        in_specs=[vmem] * 6 + [pl.BlockSpec(memory_space=pltpu.SMEM)] * 3,
+        sampler_kernel,
+        out_shape=jax.ShapeDtypeStruct(latent.shape, f32),
+        in_specs=[anywhere, vmem] + [anywhere] * 4 + [vmem] * 3
+        + [pl.BlockSpec(memory_space=pltpu.SMEM)] * 3,
         out_specs=vmem,
-        scratch_shapes=[
-            pltpu.VMEM(shape, jnp.float32),
-            pltpu.VMEM(shape, jnp.float32),
-            pltpu.VMEM(shape, jnp.bfloat16),
-            pltpu.VMEM((hops,) + shape, jnp.bfloat16),
-            pltpu.VMEM(shape, jnp.bfloat16),
-            pltpu.VMEM((hops,) + shape, jnp.bfloat16),
-        ]
-        + [pltpu.SemaphoreType.DMA((hops, blocks))] * 4,
+        scratch_shapes=[pltpu.VMEM(*each) for each in scratch]
+        + [pltpu.SemaphoreType.DMA((5,))]
+        + [pltpu.SemaphoreType.DMA((ITERS, hops, blocks))] * 4,
         compiler_params=pltpu.CompilerParams(
-            collective_id=int(last), has_side_effects=True, vmem_limit_bytes=60 * 1024 * 1024
+            collective_id=0, has_side_effects=True, vmem_limit_bytes=60 * 1024 * 1024
         ),
-        name="step_last" if last else "step",
-    )(tokens, packed, square, shift, latent, noise, *rates)
+        name="sampler",
+    )(modulation, *weights, latent, noise, *rates)
 
 
 def carried_in(last, groups, same_block, timestep, sent, increment, latent):
@@ -737,31 +842,30 @@
     rates = (drift_state, drift_denoise, noise_scale)
     same_step = [[step * groups + block for block in range(groups)] for step in range(P_SIZE)]
     same_block = [[step * groups + block for step in range(P_SIZE)] for block in range(groups)]
-    first, offset, packed, square, shift = fold(
-        own, modulation, embed_weight, space_input.T, space_output, time_input.T, time_output,
-        final_weight.T,
+    weights = (
+        embed_weight, space_input.T, space_output, time_input.T, time_output, final_weight.T
     )
+    if groups == 1:
+        return sampler(modulation, weights, initial_guess, noise_draws, rates)
+    first, offset, packed, square, shift = fold(own, modulation, *weights)
     latent = initial_guess
     for iteration in range(ITERS):
         tokens = space_block(latent, first, offset)
         last = iteration == ITERS - 1
-        if groups == 1:
-            latent = step_block(last, tokens, packed, square, shift, latent, noise_draws, rates)
-        else:
-            tokens = lax.all_to_all(
-                tokens, "tok", split_axis=1, concat_axis=0, axis_index_groups=same_step, tiled=True
-            )
-            predicted = time_block(tokens, packed, square, shift)
-            predicted = lax.all_to_all(
-                predicted, "tok", split_axis=0, concat_axis=2, axis_index_groups=same_step, tiled=True
-            )
-            rate_state, rate_denoise, rate_noise = (
-                lax.dynamic_index_in_dim(rate, timestep, 0, keepdims=False) for rate in rates
-            )
-            rate_state = rate_state + jnp.where(timestep == 0, 1.0, 0.0)
-            increment = rate_state * latent + rate_denoise * predicted + rate_noise * noise_draws
-            sent = increment.astype(jnp.bfloat16)
-            latent = carried_in(last, groups, same_block, timestep, sent, increment, latent)
+        tokens = lax.all_to_all(
+            tokens, "tok", split_axis=1, concat_axis=0, axis_index_groups=same_step, tiled=True
+        )
+        predicted = time_block(tokens, packed, square, shift)
+        predicted = lax.all_to_all(
+            predicted, "tok", split_axis=0, concat_axis=2, axis_index_groups=same_step, tiled=True
+        )
+        rate_state, rate_denoise, rate_noise = (
+            lax.dynamic_index_in_dim(rate, timestep, 0, keepdims=False) for rate in rates
+        )
+        rate_state = rate_state + jnp.where(timestep == 0, 1.0, 0.0)
+        increment = rate_state * latent + rate_denoise * predicted + rate_noise * noise_draws
+        sent = increment.astype(jnp.bfloat16)
+        latent = carried_in(last, groups, same_block, timestep, sent, increment, latent)
     return latent
 
 

time: 65.3 us -> 51.7 us (0.79)
  Pallas kernels: 63.5 us -> 50 us
    pallas_call x5 -> x1, Pallas kernels: 63.5 us -> 50 us  [sampler(): pl.pallas_call(sampler_kernel, out_shape=jax.ShapeDtypeStruct(latent.shap...]
where the time goes in v4:
time: 51.7 us; the launch traced here: 51.6 us
  Pallas kernels  50 us (97%)
  local copies, waits for them, and re-layouts  1.57 us (3%)
    pallas_call x1, Pallas kernels, sampler(): pl.pallas_call(sampler_kernel, out_shape=jax.ShapeDtypeStruct(latent.shap...  50 us
    unnamed x1, local copies, waits for them, and re-layouts  1.57 us

profile of v4, /device:TPU:0, one launch (start us, length us, event | category | flops | bytes accessed | tf_op | source)
XLA Modules:
  0.0 51.6 jit_solution(6775888334803263186)
XLA Ops:
  0.0 50.0 %sampler.1 = f32[16,16,128]{2,1,0:T(8,128)} custom-call(f32[16,8,1152]{2,1,0:T(8,128)} %table_from.1, bf16[16,1152]{1,0:T(8,128)(2,1)} %embed_ref.1, bf16[1728,1152]{1,0:T(8,128)(2,1)} %bitcast.3, bf16[576,1152]{1,0:T(8,128)(2,1)} %space_out_from.1, bf16[1728,1152]{1,0:T(8,128)(2,1)} %bitcast.4, bf16[576,1152]{1,0:T(8,128)(2,1)} %time_out_from.1, ...), custom_call_target="tpu_custom_call" | custom-call | tf_op jit(solution)/shard_map/sampler/pallas_call | solution.py:798
  50.0 1.6 %copy.14 = f32[16,16,128]{2,1,0:T(8,128)} copy(f32[16,16,128]{2,1,0:T(8,128)} %sampler.1) | data formatting | bytes 262144

commit v5 on v4

--- a/solution.py
+++ b/solution.py
@@ -19,8 +19,8 @@
 CARRIED = 2
 SPACE_LAGS = (2, 8, 6)
 FOLD_LAG = 4
-FOLD_EVERY = 3
-TIME_LAGS = (4, 8, 10, 8, 2, 48)
+FOLD_EVERY = 2
+TIME_LAGS = (4, 8, 10, 8, 2, 80)
 EPS = 1e-06
 CHANNELS = 16
 WIDE = 2 * LANES
@@ -105,77 +105,92 @@
         yield
 
 
-def fold_first(arrive, table, embed_ref, space_in_ref, first_ref, offset_ref):
-    embed = centred(embed_ref[...].astype(jnp.float32))
-    features = embed.shape[1]
+def fold_tasks(
+    lag, arrive, state, table, embed_ref, space_in_ref, space_out_ref, time_in_ref, time_out_ref,
+    final_ref, first_ref, offset_ref, packed_ref, square_ref, shift_ref, lines_ref,
+):
+    f32 = jnp.float32
+    bf16 = jnp.bfloat16
+    features = embed_ref.shape[1]
+    embed = centred(embed_ref[...].astype(f32))
+    state.update(mixed={}, lines=set())
 
     def zeros(rows, width=features):
-        return jnp.zeros((rows, width), jnp.float32)
-
-    arrive("table")
-    lines = stack(*halves(embed * (1.0 + table(1))))
-    tail = stack(*(half.astype(jnp.float32) for half in halves(stack(table(0), zeros(7)))))
-    arrive("space_in")
-    folded = dot_rows(stack(lines, tail.astype(jnp.bfloat16)), space_in_ref[...])
-    lat = folded[:CHANNELS] + folded[CHANNELS : 2 * CHANNELS]
-    const = folded[2 * CHANNELS : 2 * CHANNELS + 8] + folded[2 * CHANNELS + 8 :]
-
-    def part(values, which):
-        return values[:, which * INNER : (which + 1) * INNER]
-
-    def fine(rows, side):
+        return jnp.zeros((rows, width), f32)
+
+    def fine_parts(rows, side):
         high, low = halves(rows)
         side_high, side_low = halves(side)
-        both = dot_rows(high, stack(side_high, side_low))
-        return both[:, :LANES] + both[:, LANES:] + dot_rows(low, side_high)
+        return dot_rows(high, stack(side_high, side_low)), dot_rows(low, side_high)
+
+    def fine_sum(both, rest):
+        return both[:, :LANES] + both[:, LANES:] + rest
 
     def side_of(rows, point):
         width = rows.shape[1]
         return stack(rows, rows, point, zeros(7, width), zeros(LANES - 2 * CHANNELS - 8, width))
 
-    query, key, value = (part(lat, which) for which in range(3))
-    query_c, key_c, value_c = (part(const, which)[:1] for which in range(3))
-    key_side, query_side = side_of(key, key_c), side_of(query, query_c)
-    scores = fine(stack(by_head(query, "hc"), by_head(query_c, "ch")) * SCALE, key_side)
-    key_square = fine(stack(by_head(key, "ch"), by_head(key_c, "ch")) * (1.0 / HD), key_side)
-    query_square = fine(stack(by_head(query, "ch"), by_head(query_c, "ch")) * (1.0 / HD), query_side)
-    gram = fine(embed, side_of(embed, zeros(1))) * (1.0 / features)
-    first = stack(scores, key_square[:ROWS_T], query_square[:ROWS_T], gram, zeros(8, LANES))
-    high, low = halves(first)
-    upper = lane_of(first.shape) < CHANNELS
-    chosen = jnp.where(upper, high.astype(jnp.float32), low.astype(jnp.float32))
-    first_ref[...] = chosen[:, : 2 * CHANNELS].astype(jnp.bfloat16)
-    point = 2 * CHANNELS
-    offset_ref[: ROWS_T + 8] = jnp.broadcast_to(scores[:, point : point + 1], (ROWS_T + 8, LANES))
-    for index, square in enumerate((key_square, query_square)):
-        start = ROWS_T + 8 + index * (ROWS_T + 8)
-        offset_ref[start : start + ROWS_T] = jnp.broadcast_to(
-            2.0 * square[:ROWS_T, point : point + 1], (ROWS_T, LANES)
-        )
-        offset_ref[start + ROWS_T : start + ROWS_T + 8] = jnp.broadcast_to(
-            square[ROWS_T:, point : point + 1], (8, LANES)
-        )
-    values = stack(*halves(by_head(value, "hc")))
-    tail = stack(*(half.astype(jnp.float32) for half in halves(stack(value_c, zeros(7, INNER)))))
-    return embed, stack(values, tail.astype(jnp.bfloat16))
-
-
-def fold_tasks(
-    lag, arrive, table, embed, values, space_out_ref, time_in_ref, time_out_ref, final_ref,
-    packed_ref, square_ref, shift_ref, lines_ref,
-):
-    f32 = jnp.float32
-    bf16 = jnp.bfloat16
-    features = embed.shape[1]
-    state = {"mixed": {}, "lines": set()}
-
-    def zeros(rows, width=features):
-        return jnp.zeros((rows, width), f32)
+    def first_task():
+        arrive("table")
+        lines = stack(*halves(embed * (1.0 + table(1))))
+        tail = stack(*(half.astype(f32) for half in halves(stack(table(0), zeros(7)))))
+        left = stack(lines, tail.astype(bf16))
+        folded = []
+        for which in range(3):
+            arrive(("space_in", which))
+            folded.append(dot_rows(left, space_in_ref[which * INNER : (which + 1) * INNER]))
+            yield
+        yield from pause(lag)
+        query, key, value = (
+            own[:CHANNELS] + own[CHANNELS : 2 * CHANNELS] for own in folded
+        )
+        query_c, key_c, value_c = (
+            (own[2 * CHANNELS : 2 * CHANNELS + 8] + own[2 * CHANNELS + 8 :])[:1] for own in folded
+        )
+        key_side, query_side = side_of(key, key_c), side_of(query, query_c)
+        scores = fine_parts(stack(by_head(query, "hc"), by_head(query_c, "ch")) * SCALE, key_side)
+        yield
+        key_square = fine_parts(
+            stack(by_head(key, "ch"), by_head(key_c, "ch")) * (1.0 / HD), key_side
+        )
+        yield
+        query_square = fine_parts(
+            stack(by_head(query, "ch"), by_head(query_c, "ch")) * (1.0 / HD), query_side
+        )
+        gram = fine_parts(embed, side_of(embed, zeros(1)))
+        yield
+        values = stack(*halves(by_head(value, "hc")))
+        tail = stack(*(half.astype(f32) for half in halves(stack(value_c, zeros(7, INNER)))))
+        state["values"] = stack(values, tail.astype(bf16))
+        yield from pause(lag)
+        scores, key_square, query_square = (
+            fine_sum(*each) for each in (scores, key_square, query_square)
+        )
+        gram = fine_sum(*gram) * (1.0 / features)
+        first = stack(scores, key_square[:ROWS_T], query_square[:ROWS_T], gram, zeros(8, LANES))
+        high, low = halves(first)
+        upper = lane_of(first.shape) < CHANNELS
+        chosen = jnp.where(upper, high.astype(f32), low.astype(f32))
+        first_ref[...] = chosen[:, : 2 * CHANNELS].astype(bf16)
+        point = 2 * CHANNELS
+        offset_ref[: ROWS_T + 8] = jnp.broadcast_to(
+            scores[:, point : point + 1], (ROWS_T + 8, LANES)
+        )
+        for index, square in enumerate((key_square, query_square)):
+            start = ROWS_T + 8 + index * (ROWS_T + 8)
+            offset_ref[start : start + ROWS_T] = jnp.broadcast_to(
+                2.0 * square[:ROWS_T, point : point + 1], (ROWS_T, LANES)
+            )
+            offset_ref[start + ROWS_T : start + ROWS_T + 8] = jnp.broadcast_to(
+                square[ROWS_T:, point : point + 1], (8, LANES)
+            )
+        state["first"] = True
 
     def mixed_task(start):
+        yield from wait_for(state, "values")
         if start == 0:
             arrive("space_out")
-        own = dot(values, space_out_ref[:, start : min(start + WIDE, features)])
+        own = dot(state["values"], space_out_ref[:, start : min(start + WIDE, features)])
         yield from pause(lag)
         state["mixed"][start] = own
 
@@ -239,7 +254,7 @@
     tiles = lines_ref.shape[0] // WIDE
 
     def square_task(column, row):
-        while len(state["lines"]) < 2 + BASE // LANES:
+        while len(state["lines"]) < 2 + BASE // LANES - (column > 0) or column == 0 and "tokens" not in state["lines"]:
             yield
         other = lines_ref[column * WIDE : (column + 1) * WIDE]
         if column == 0:
@@ -260,12 +275,19 @@
             (block * gain).astype(bf16)
         )
 
-    starts = range(0, features, WIDE)
-    yield from (mixed_task(start) for start in starts)
-    yield rows_task()
-    yield from (lines_task(start) for start in range(0, BASE + 1, LANES))
-    yield from (packed_task(start) for start in range(0, 3 * INNER, WIDE))
-    yield from (square_task(column, row) for column in range(tiles) for row in range(column, tiles))
+    def ordered():
+        packed = [packed_task(start) for start in range(0, 3 * INNER, WIDE)]
+        early = [square_task(column, row) for column in range(1, tiles) for row in range(column, tiles)]
+        mixed = [mixed_task(start) for start in range(0, features, WIDE)]
+        yield from mixed[:2]
+        yield from early
+        yield from mixed[2:]
+        yield rows_task()
+        yield from packed
+        yield from (square_task(0, row) for row in range(tiles))
+
+    lines = [lines_task(start) for start in range(0, BASE + 1, LANES)]
+    return [first_task(), *lines], ordered()
 
 
 def fold_kernel(
@@ -278,16 +300,14 @@
     def arrive(name):
         pass
 
-    embed, values = fold_first(arrive, table, embed_ref, space_in_ref, first_ref, offset_ref)
-    interleave(
-        fold_tasks(
-            3, arrive, table, embed, values, space_out_ref, time_in_ref, time_out_ref, final_ref,
-            packed_ref, square_ref, shift_ref, lines_ref,
-        )
+    ahead, others = fold_tasks(
+        3, arrive, {}, table, embed_ref, space_in_ref, space_out_ref, time_in_ref, time_out_ref,
+        final_ref, first_ref, offset_ref, packed_ref, square_ref, shift_ref, lines_ref,
     )
-
-
-def space_tasks(lags, latent_ref, first_ref, offset_ref, token_ref):
+    interleave([*ahead, *others])
+
+
+def space_tasks(lags, ready, latent_ref, first_ref, offset_ref, token_ref):
     frames, channels, spatial = latent_ref.shape
     bf16 = jnp.bfloat16
     f32 = jnp.float32
@@ -304,6 +324,7 @@
         return stack(latent, latent)
 
     def couple_task(frame):
+        yield from wait_for(ready, "first")
         own = range(frame, min(frame + 2, frames))
         product = dot(first_ref[...], beside(*(twice(index) for index in own)))
         yield from pause(lags[0])
@@ -392,7 +413,7 @@
 
 
 def space_kernel(lags, *refs):
-    interleave(space_tasks(lags, *refs))
+    interleave(space_tasks(lags, {"first": True}, *refs))
 
 
 def regrid(chunks):
@@ -562,14 +583,20 @@
     plane, seat = timestep // SIDE, timestep % SIDE
     hops = range(1, SIDE)
 
+    def rows_of(which):
+        return slice(which * INNER, (which + 1) * INNER)
+
     loads = {
         name: pltpu.make_async_copy(source, target, load_sem.at[index])
         for index, (name, source, target) in enumerate(
             (
                 ("table", table_from.at[timestep], table_ref),
-                ("space_in", space_in_from, space_in_ref),
+                *(
+                    (("space_in", which), space_in_from.at[rows_of(which)], space_in_ref.at[rows_of(which)])
+                    for which in range(3)
+                ),
+                ("time_out", time_out_from, time_out_ref),
                 ("space_out", space_out_from, space_out_ref),
-                ("time_out", time_out_from, time_out_ref),
                 ("time_in", time_in_from, time_in_ref),
             )
         )
@@ -603,7 +630,7 @@
     for target, source in ((running_ref, latent_ref), (fresh_ref, noise_ref)):
         for index, own in enumerate(regrid([source[frame] for frame in range(frames)])):
             target[index] = own
-    embed, values = fold_first(arrive, table, embed_ref, space_in_ref, first_ref, offset_ref)
+    state = {}
 
     def copy(source, target, send, receive, to):
         return pltpu.make_async_remote_copy(
@@ -615,13 +642,14 @@
     for iteration in range(ITERS):
         last = iteration == ITERS - 1
         source_ref = own_ref if iteration else latent_ref
-        spread = space_tasks(SPACE_LAGS, source_ref, first_ref, offset_ref, token_ref)
+        spread = space_tasks(SPACE_LAGS, state, source_ref, first_ref, offset_ref, token_ref)
         if iteration == 0:
-            others = fold_tasks(
-                FOLD_LAG, arrive, table, embed, values, space_out_ref, time_in_ref, time_out_ref,
-                final_ref, packed_ref, square_ref, shift_ref, lines_ref,
+            ahead, others = fold_tasks(
+                FOLD_LAG, arrive, state, table, embed_ref, space_in_ref, space_out_ref, time_in_ref,
+                time_out_ref, final_ref, first_ref, offset_ref, packed_ref, square_ref, shift_ref,
+                lines_ref,
             )
-            spread = merged(spread, others, FOLD_EVERY)
+            spread = [*ahead, *merged(spread, others, FOLD_EVERY)]
         interleave(spread)
         if iteration == 0:
             pl.semaphore_wait(barrier, 2 * (SIDE - 1))
@@ -802,7 +830,7 @@
         + [pl.BlockSpec(memory_space=pltpu.SMEM)] * 3,
         out_specs=vmem,
         scratch_shapes=[pltpu.VMEM(*each) for each in scratch]
-        + [pltpu.SemaphoreType.DMA((5,))]
+        + [pltpu.SemaphoreType.DMA((7,))]
         + [pltpu.SemaphoreType.DMA((ITERS, hops, blocks))] * 4,
         compiler_params=pltpu.CompilerParams(
             collective_id=0, has_side_effects=True, vmem_limit_bytes=60 * 1024 * 1024

time: 51.7 us -> 49.6 us (0.959)
  Pallas kernels: 50 us -> 47.9 us
    pallas_call x1, Pallas kernels: 50 us -> 47.9 us  [sampler(): pl.pallas_call(sampler_kernel, out_shape=jax.ShapeDtypeStruct(latent.shap...]
where the time goes in v5:
time: 49.6 us; the launch traced here: 49.5 us
  Pallas kernels  47.9 us (97%)
  local copies, waits for them, and re-layouts  1.57 us (3%)
    pallas_call x1, Pallas kernels, sampler(): pl.pallas_call(sampler_kernel, out_shape=jax.ShapeDtypeStruct(latent.shap...  47.9 us
    unnamed x1, local copies, waits for them, and re-layouts  1.57 us

profile of v5, /device:TPU:0, one launch (start us, length us, event | category | flops | bytes accessed | tf_op | source)
XLA Modules:
  0.0 49.5 jit_solution(8467949771661397615)
XLA Ops:
  0.0 47.9 %sampler.1 = f32[16,16,128]{2,1,0:T(8,128)} custom-call(f32[16,8,1152]{2,1,0:T(8,128)} %table_from.1, bf16[16,1152]{1,0:T(8,128)(2,1)} %embed_ref.1, bf16[1728,1152]{1,0:T(8,128)(2,1)} %bitcast.3, bf16[576,1152]{1,0:T(8,128)(2,1)} %space_out_from.1, bf16[1728,1152]{1,0:T(8,128)(2,1)} %bitcast.4, bf16[576,1152]{1,0:T(8,128)(2,1)} %time_out_from.1, ...), custom_call_target="tpu_custom_call" | custom-call | tf_op jit(solution)/shard_map/sampler/pallas_call | solution.py:826
  47.9 1.6 %copy.14 = f32[16,16,128]{2,1,0:T(8,128)} copy(f32[16,16,128]{2,1,0:T(8,128)} %sampler.1) | data formatting | bytes 262144

commit v6 on v5

--- a/solution.py
+++ b/solution.py
@@ -578,7 +578,7 @@
 ):
     f32 = jnp.float32
     bf16 = jnp.bfloat16
-    frames = latent_ref.shape[0]
+    frames, _, positions = latent_ref.shape
     timestep = lax.axis_index("tok")
     plane, seat = timestep // SIDE, timestep % SIDE
     hops = range(1, SIDE)
@@ -610,6 +610,7 @@
     def in_seat(hop):
         return {"tok": (plane + hop) % SIDE * SIDE + seat}
 
+    plane_ref[...] = jnp.zeros_like(plane_ref)
     barrier = pltpu.get_barrier_semaphore()
     for hop in hops:
         for target in (in_plane(hop), in_seat(hop)):
@@ -690,10 +691,15 @@
                 )
                 for hop in hops
             ]
-            for part in planes:
-                part.start()
-            started.append((own, planes))
-            sent.extend(parts + planes)
+            only = True
+            for hop, part in zip(hops, planes):
+                if only:
+                    pl.when(plane + hop < SIDE)(part.start)
+                else:
+                    part.start()
+            started.append((own, planes, only))
+            sent.extend((0, part) for part in parts)
+            sent.extend((hop if only else 0, part) for hop, part in zip(hops, planes))
 
         def after(group, parts):
             if (group + 1) % CARRIED == 0:
@@ -702,9 +708,12 @@
 
         interleave(time_tasks(TIME_LAGS, token_ref, packed_ref, square_ref, finish, after))
         chunks = []
-        for own, planes in started:
-            for part in planes:
-                part.wait_recv()
+        for own, planes, only in started:
+            for hop, part in zip(hops, planes):
+                if only:
+                    pl.when(plane >= hop)(part.wait_recv)
+                else:
+                    part.wait_recv()
             for index in range(own.start, own.stop):
                 before = jnp.zeros(latent_ref.shape[1:], f32)
                 for hop in hops:
@@ -720,8 +729,11 @@
         target_ref = out_ref if last else own_ref
         for frame, own in enumerate(regrid(chunks)):
             target_ref[frame] = own
-    for part in sent:
-        part.wait_send()
+    for hop, part in sent:
+        if hop:
+            pl.when(plane + hop < SIDE)(part.wait_send)
+        else:
+            part.wait_send()
 
 
 def whole(array):

time: 49.6 us -> 43.2 us (0.87)
  the two profiles are of different devices: /device:TPU:0 before, /device:TPU:24 now
where the time goes in v6:
time: 43.2 us; the launch traced here: 43 us
  Pallas kernels  41.5 us (96%)
  local copies, waits for them, and re-layouts  1.57 us (4%)
    pallas_call x1, Pallas kernels, sampler(): pl.pallas_call(sampler_kernel, out_shape=jax.ShapeDtypeStruct(latent.shap...  41.5 us
    unnamed x1, local copies, waits for them, and re-layouts  1.57 us

profile of v6, /device:TPU:24, one launch (start us, length us, event | category | flops | bytes accessed | tf_op | source)
XLA Modules:
  0.0 43.0 jit_solution(13909960049351966285)
XLA Ops:
  0.0 41.5 %sampler.1 = f32[16,16,128]{2,1,0:T(8,128)} custom-call(f32[16,8,1152]{2,1,0:T(8,128)} %table_from.1, bf16[16,1152]{1,0:T(8,128)(2,1)} %embed_ref.1, bf16[1728,1152]{1,0:T(8,128)(2,1)} %bitcast.3, bf16[576,1152]{1,0:T(8,128)(2,1)} %space_out_from.1, bf16[1728,1152]{1,0:T(8,128)(2,1)} %bitcast.4, bf16[576,1152]{1,0:T(8,128)(2,1)} %time_out_from.1, ...), custom_call_target="tpu_custom_call" | custom-call | tf_op jit(solution)/shard_map/sampler/pallas_call | solution.py:838
  41.5 1.6 %copy.14 = f32[16,16,128]{2,1,0:T(8,128)} copy(f32[16,16,128]{2,1,0:T(8,128)} %sampler.1) | data formatting | bytes 262144
